TPU v7x, 256 devices: a whole 4x4x8 slice. The times are simulated.
256 devices in a mesh: chan: 8 (over x, core), filt: 32 (over y, z).
Axes of the slice: x: 4, y: 4, z: 8, core: 2. Of those that a mesh axis runs over, the one named last changes fastest.
Arguments:
- inputs: bfloat16 [1, 64, 128, 1024], P(None, 'filt', None, 'chan'), may hold values from -6 to 6
- weights: bfloat16 [3, 3, 1024, 1024], P(None, None, 'filt', 'chan'), may hold values from -0.0625 to 0.0625
- cotangent: bfloat16 [1, 64, 1024, 128], P(None, 'chan', 'filt'), may hold values from -6 to 6
Outputs:
- outputs: bfloat16 [1, 64, 1024, 128], P(None, 'chan', 'filt')
- input_grad: bfloat16 [1, 64, 128, 1024], P(None, 'filt', None, 'chan')
- weight_grad: float32 [3, 3, 1024, 1024], P(None, None, 'filt', 'chan')
All inputs are finite; a program needn't handle non-finite values.
Results may differ from a plain program's by a relative error of at most 0.001.
Values may be sent and summed in bfloat16 or wider, within the bound.
A program may use at most 128 MiB of HBM per device.

v0:
```python
import math

import jax
import jax.numpy as jnp
from jax import lax
from jax.sharding import PartitionSpec as P


def backward_taps(padded, kernel, row_count, col_count):
    summed = None
    for tap_row in range(3):
        for tap_col in range(3):
            source = padded[
                :, 2 - tap_row : 2 - tap_row + row_count, :, 2 - tap_col : 2 - tap_col + col_count
            ]
            product = jnp.einsum(
                "bhfw,fc->bhwc",
                source,
                kernel[tap_row, tap_col],
                preferred_element_type=jnp.float32,
            )
            summed = product if summed is None else summed + product
    return summed


def body(inputs, weights, cotangent):
    gathered = lax.all_gather(inputs, "filt", axis=1, tiled=True)
    cot_all = lax.all_gather(cotangent, "chan", axis=1, tiled=True)
    row_count = gathered.shape[1]
    col_count = gathered.shape[2]
    padded_in = jnp.pad(gathered, ((0, 0), (1, 1), (1, 1), (0, 0)))
    norm_factor = 1.0 / math.sqrt(gathered.shape[0] * row_count * col_count)
    summed_out = None
    grad_taps = []
    for tap_row in range(3):
        for tap_col in range(3):
            source = padded_in[:, tap_row : tap_row + row_count, tap_col : tap_col + col_count, :]
            product = jnp.einsum(
                "bhwc,fc->bhwf",
                source,
                weights[tap_row, tap_col],
                preferred_element_type=jnp.float32,
            )
            summed_out = product if summed_out is None else summed_out + product
            grad_taps.append(
                jnp.einsum("bhwc,bhfw->fc", source, cot_all, preferred_element_type=jnp.float32)
                * norm_factor
            )
    partial_out = jnp.transpose(summed_out, (0, 1, 3, 2))
    outputs = lax.psum_scatter(partial_out, "chan", scatter_dimension=1, tiled=True).astype(
        jnp.bfloat16
    )
    weight_grad = jnp.stack(grad_taps).reshape(3, 3, weights.shape[2], weights.shape[3])
    padded_cot = jnp.pad(cot_all, ((0, 0), (1, 1), (0, 0), (1, 1)))
    partial_grad = backward_taps(padded_cot, weights, row_count, col_count)
    input_grad = lax.psum_scatter(partial_grad, "filt", scatter_dimension=1, tiled=True).astype(
        jnp.bfloat16
    )
    return (outputs, input_grad, weight_grad)


def solution(mesh):
    return jax.shard_map(
        body,
        mesh=mesh,
        in_specs=(
            P(None, "filt", None, "chan"),
            P(None, None, "filt", "chan"),
            P(None, "chan", "filt", None),
        ),
        out_specs=(
            P(None, "chan", "filt", None),
            P(None, "filt", None, "chan"),
            P(None, None, "filt", "chan"),
        ),
        check_vma=False,
    )
```

profile of v0, /device:TPU:1, one launch (start us, length us, event | category | flops | bytes accessed | tf_op | source)
XLA Modules:
  0.0 364.4 jit_solution(7794976326158176993)
XLA Ops:
  7.2 0.0 all-gather.2.cloned.1.call-start
  7.2 0.7 all-gather.2.cloned.1.call-update
  7.9 0.0 reduce-scatter.3.cloned.1.call-start
  7.9 16.4 %all_gather.7 = bf16[1,64,32,128]{3,2,0,1:T(8,128)(2,1)S(1)} all-gather(bf16[1,8,32,128]{3,2,0,1:T(8,128)(2,1)} %bitcast.402), channel_id=1, replica_groups=mesh['chan'=8,'filt'=32] {'chan'}, dimensions={1}, use_global_device_ids=true | all-gather | bytes 589824 | tf_op jit(solution)/shard_map/all_gather | solution.py:28
  24.3 0.0 copy-start.4
  24.3 3.8 %fusion.188 = f32[64,128,128]{2,1,0:T(8,128)} fusion(bf16[1,64,32,128]{3,2,1,0:T(8,128)(2,1)S(1)} %bitcast.394, bf16[3,3,32,128]{3,2,1,0:T(8,128)(2,1)} %param.4), kind=kOutput, calls=%fused_computation.107 | convolution fusion | flops 67108864 | bytes 4726784 | tf_op jit(solution)/shard_map/bhfw,fc->bhwc/dot_general | solution.py:16
  28.1 0.0 copy-done.4
  28.1 2.7 fusion.191
  30.8 3.0 fusion.194
  33.8 3.0 fusion.197
  36.9 3.0 fusion.200
  39.9 48.0 %all-gather.2.cloned.1.call-done = bf16[1,64,128,128]{3,2,0,1:T(8,128)(2,1)} async-done(((bf16[1,2,128,128]{3,2,0,1:T(8,128)(2,1)}), bf16[1,64,128,128]{3,2,0,1:T(8,128)(2,1)}) %all-gather.2.cloned.1.call-update) | async-done | bytes 2097168 | tf_op jit(solution)/shard_map/all_gather | solution.py:27
  87.8 0.0 copy-start
  87.8 2.5 fusion.26
  90.3 0.0 copy-done
  90.4 0.8 fusion.30
  91.2 0.8 fusion.10
  92.0 0.8 fusion.2
  92.8 0.8 fusion.55
  93.7 0.8 fusion.18
  94.5 0.8 fusion.61
  95.3 0.8 fusion.67
  96.2 1.8 fusion.76
  98.0 0.0 reduce-scatter.3.cloned.1.call-update
  98.0 0.2 reduce-scatter.5.cloned.1.call-start
  98.3 0.0 copy-start.3
  98.3 3.0 fusion.203
  101.3 0.0 copy-start.2
  101.3 2.7 fusion.206
  104.0 0.0 copy-start.1
  104.0 2.7 fusion.219
  106.7 0.0 copy-done.3
  106.7 0.0 copy-done.2
  106.7 0.6 copy-done.1
  107.4 10.6 %add_bitcast_fusion = f32[1,64,128,128]{3,2,1,0:T(8,128)} fusion(f32[64,128,128]{2,1,0:T(8,128)} %fusion.206, f32[64,128,128]{2,1,0:T(8,128)} %fusion.203, f32[64,128,128]{2,1,0:T(8,128)} %fusion.200, f32[64,128,128]{2,1,0:T(8,128)} %fusion.219, f32[64,128,128]{2,1,0:T(8,128)} %fusion.197, f32[64,128,128]{2,1,0:T(8,128)S(1)} %copy-done.3, ...), kind=kOutput, calls=%fused_computation | convolution fusion | flops 75497472 | bytes 38281216 | tf_op jit(solution)/shard_map/bhfw,fc->bhwc/dot_general | solution.py:16
  118.0 0.0 reduce-scatter.5.cloned.1.call-update
  118.1 0.7 fusion.175
  118.8 0.5 fusion.166
  119.2 0.8 fusion.157
  120.0 0.8 fusion.148
  120.8 0.5 fusion.184
  121.3 0.8 fusion.139
  122.0 0.8 fusion.130
  122.8 0.5 fusion.121
  123.3 0.8 fusion.112
  124.0 0.0 copy-start.5
  124.1 8.4 %reduce-scatter.3.cloned.1.call-done = f32[1,8,32,128]{3,2,1,0:T(8,128)} async-done(((f32[1,64,32,128]{3,2,1,0:T(8,128)}), f32[1,8,32,128]{3,2,1,0:T(8,128)}) %reduce-scatter.3.cloned.1.call-update) | async-done | bytes 131088 | tf_op jit(solution)/shard_map/reduce_scatter | solution.py:50
  132.5 1.5 convert_element_type.10
  134.0 222.3 %reduce-scatter.5.cloned.1.call-done = f32[1,2,128,128]{3,2,1,0:T(8,128)} async-done(((f32[1,64,128,128]{3,2,1,0:T(8,128)}), f32[1,2,128,128]{3,2,1,0:T(8,128)}) %reduce-scatter.5.cloned.1.call-update) | async-done | bytes 131088 | tf_op jit(solution)/shard_map/reduce_scatter | solution.py:56
  356.3 1.5 convert_element_type.11
  357.9 0.0 copy-done.5
Async XLA Ops:
  7.2 80.6 %all-gather.2.cloned.1.call-start = ((), (), s32[]{:S(2)}) async-start(), calls=%async_computation.2 | async-start | bytes 2162688 | tf_op jit(solution)/shard_map/all_gather | solution.py:27
  7.9 124.6 %reduce-scatter.3.cloned.1.call-start = ((), (), s32[]{:S(2)}) async-start(), calls=%async_computation.3 | async-start | bytes 1179648 | tf_op jit(solution)/shard_map/reduce_scatter | solution.py:50
  24.3 3.8 %copy-start.4 = (bf16[3,3,32,128]{3,2,1,0:T(8,128)(2,1)S(1)}, bf16[3,3,32,128]{3,2,1,0:T(8,128)(2,1)}, u32[]{:S(2)}) copy-start(bf16[3,3,32,128]{3,2,1,0:T(8,128)(2,1)} %param.4) | copy-start | bytes 221188
  87.8 2.6 copy-start
  98.0 258.3 %reduce-scatter.5.cloned.1.call-start = ((), (), s32[]{:S(2)}) async-start(), calls=%async_computation.4 | async-start | bytes 4325376 | tf_op jit(solution)/shard_map/reduce_scatter | solution.py:56
  98.3 8.5 %copy-start.3 = (f32[64,128,128]{2,1,0:T(8,128)S(1)}, f32[64,128,128]{2,1,0:T(8,128)}, u32[]{:S(2)}) copy-start(f32[64,128,128]{2,1,0:T(8,128)} %fusion.194) | copy-start | bytes 12582916
  101.3 5.5 %copy-start.2 = (f32[64,128,128]{2,1,0:T(8,128)S(1)}, f32[64,128,128]{2,1,0:T(8,128)}, u32[]{:S(2)}) copy-start(f32[64,128,128]{2,1,0:T(8,128)} %fusion.191) | copy-start | bytes 12582916
  104.0 3.4 copy-start.1
  124.0 233.8 %copy-start.5 = (f32[9,32,128]{2,1,0:T(8,128)}, f32[9,32,128]{2,1,0:T(8,128)S(1)}, u32[]{:S(2)}) copy-start(f32[9,32,128]{2,1,0:T(8,128)S(1)} %fusion.112) | copy-start | bytes 442372
Sparse Core Ops, SparseCore 0:
  10.6 77.1 all-gather.1
  98.1 34.2 reduce-scatter.2
  136.4 219.8 reduce-scatter.4
where the time goes:
time: 369 us; the launch traced here: 364 us
  waiting for transfers between devices  279 us (76%)
  matrix products  50.8 us (14%)
  blocking collectives  16.4 us (4%)
  between operations  13.8 us (4%)
    reduce_scatter x1, waiting for transfers between devices, body(): lax.psum_scatter(partial_grad, 'filt', scatter_dimension=1, tiled=True)  222 us
    all_gather x1, waiting for transfers between devices, body(): gathered = lax.all_gather(inputs, 'filt', axis=1, tiled=True)  48 us
    dot_general x9, matrix products, backward_taps(): jnp.einsum('bhfw,fc->bhwc', source, kernel[tap_row, tap_col], preferred_e...  34.7 us
    all_gather x1, blocking collectives, body(): cot_all = lax.all_gather(cotangent, 'chan', axis=1, tiled=True)  16.4 us
    dot_general x9, matrix products, body(): jnp.einsum('bhwc,fc->bhwf', source, weights[tap_row, tap_col], preferred_...  10.2 us
    reduce_scatter x1, waiting for transfers between devices, body(): lax.psum_scatter(partial_out, 'chan', scatter_dimension=1, tiled=True)  8.43 us
  transfers between devices with their start and end apart: 3, of which 3 were waited for; matrix products, arithmetic and copies ran while one was open for 12% of the time, Pallas kernels for 0%

commit v1 on v0

v1 whole, which is shorter than its diff:
```python
import functools
import math

import jax
import jax.numpy as jnp
from jax import lax
from jax.experimental import pallas as pl
from jax.experimental.pallas import tpu as pltpu
from jax.sharding import PartitionSpec as P

MESH = pl.DeviceIdType.MESH
BF16 = jnp.bfloat16
F32 = jnp.float32

NX, NY, NZ = 4, 4, 8
LANES = 128

SEM_X = 0
SEM_W = 8
SEM_G = 12
SEM_T = 16
SEM_C = 18
SEM_DX = 22
SEM_DW = 30
SEM_OC = 34
SEM_O = 35
SEM_OH = 39
SEM_OT = 40
N_SEMS = 41


def kernel(
    norm,
    x_in, w_in, g_in,
    out_o, dx_o, dw_o,
    xg, wg, gg, x3, y3, dyn, wf, wb,
    pdx, rdx, acc, pdw, rdw, po, rk, ro, rh, ob, orx,
    ss, rs,
):
    chan = lax.axis_index("chan")
    filt = lax.axis_index("filt")
    x, k = lax.div(chan, 2), lax.rem(chan, 2)
    y, z = lax.div(filt, NZ), lax.rem(filt, NZ)

    def dev(dx, dk, dy, dz):
        return (dx * 2 + dk, dy * NZ + dz)

    def mod(v, n):
        return lax.rem(v + n, n)

    x_right, x_left = dev(mod(x + 1, NX), k, y, z), dev(mod(x - 1, NX), k, y, z)
    y_right, y_left = dev(x, k, mod(y + 1, NY), z), dev(x, k, mod(y - 1, NY), z)
    z_right, z_left = dev(x, k, y, mod(z + 1, NZ)), dev(x, k, y, mod(z - 1, NZ))
    other = dev(x, 1 - k, y, z)
    swap = dev(y, k, x, z)
    off_diag = x != y
    step = 2 * k - 1
    halo_to = dev(y, 1 - k, mod(x + step, NY), z)
    halo_from = dev(mod(y + step, NX), 1 - k, x, z)
    edge = dev(x, 1 - k, mod(y + step, NY), z)

    barrier = pltpu.get_barrier_semaphore()
    for peer in (
        x_right, x_left, y_right, y_left, z_right, z_left, other, halo_to, halo_from, edge,
    ):
        pl.semaphore_signal(barrier, inc=1, device_id=peer, device_id_type=MESH)

    @pl.when(off_diag)
    def _():
        pl.semaphore_signal(barrier, inc=1, device_id=swap, device_id_type=MESH)

    xg[z] = x_in[...]
    wg[y] = w_in[...]
    pl.semaphore_wait(barrier, jnp.where(off_diag, 11, 10))

    sent = []

    def rcopy(src, dst, idx, target):
        return pltpu.make_async_remote_copy(
            src_ref=src, dst_ref=dst, send_sem=ss.at[idx], recv_sem=rs.at[idx],
            device_id=target, device_id_type=MESH,
        )

    def push(src, dst, idx, target):
        copy = rcopy(src, dst, idx, target)
        copy.start()
        sent.append(copy)

    def landed(dst, idx):
        rcopy(dst, dst, idx, other).wait_recv()

    def gather(buf, own, pos, n, right, left, base, half):
        last = n // 2

        def send(s):
            for d in range(2):
                block = mod(pos - s + 1, n) if d == 0 else mod(pos + s - 1, n)
                src = own if s == 1 else buf.at[block]
                dst = buf.at[block]
                if s == last:
                    src, dst = half(src, d), half(dst, d)
                push(src, dst, base + d * last + s - 1, right if d == 0 else left)

        def recv(s):
            for d in range(2):
                block = mod(pos - s, n) if d == 0 else mod(pos + s, n)
                dst = buf.at[block]
                if s == last:
                    dst = half(dst, d)
                landed(dst, base + d * last + s - 1)

        return send, recv

    def scatter(part, got, pos, n, right, left, base, half):
        last = n // 2

        def dest(t, d):
            away = last + 1 - t
            return mod(pos + away, n) if d == 0 else mod(pos - away, n)

        def send(t):
            for d in range(2):
                src, dst = part(dest(t, d)), got.at[d, t - 1]
                if t == 1:
                    src, dst = half(src, d), half(dst, d)
                push(src, dst, base + d * last + t - 1, right if d == 0 else left)

        def recv(t):
            for d in range(2):
                dst = got.at[d, t - 1]
                if t == 1:
                    dst = half(dst, d)
                landed(dst, base + d * last + t - 1)

        def add(t):
            for d in range(2):
                into, term = part(dest(t + 1, d)), got.at[d, t - 1]
                if t == 1:
                    into, term = half(into, d), half(term, d)
                into[...] += term[...]

        def advance(t):
            recv(t)
            add(t)
            send(t + 1)

        return send, recv, advance

    first = lambda ref, d: ref.at[d]
    x_send, x_recv = gather(xg, x_in, z, NZ, z_right, z_left, SEM_X, first)
    w_send, w_recv = gather(
        wg, w_in, y, NY, y_right, y_left, SEM_W, lambda ref, d: ref.at[:, :, pl.ds(16 * d, 16)]
    )
    gk = gg.at[k]
    g_send, g_recv = gather(
        gk, gk.at[x], x, NX, x_right, x_left, SEM_G, lambda ref, d: ref.at[:, pl.ds(16 * d, 16)]
    )
    dx_send, dx_recv, dx_advance = scatter(
        lambda i: pdx.at[i + 1], rdx, z, NZ, z_right, z_left, SEM_DX, first
    )
    dw_send, dw_recv, dw_advance = scatter(
        lambda i: pdw.at[i], rdw, y, NY, y_right, y_left, SEM_DW, first
    )
    pk = po.at[k]
    o_send, o_recv, o_advance = scatter(
        lambda i: pk.at[i], ro, x, NX, x_right, x_left, SEM_O, first
    )

    main_dst = gg.at[k, y, pl.ds(1 - k, 8)]

    @pl.when(off_diag)
    def _():
        rcopy(g_in, main_dst, SEM_T, swap).start()

    @pl.when(jnp.logical_not(off_diag))
    def _():
        pltpu.make_async_copy(g_in, main_dst, rs.at[SEM_T]).start()

    push(g_in.at[7 * k], gg.at[1 - k, y, 8 * (1 - k)], SEM_T + 1, halo_to)
    w_send(1)
    x_send(1)

    own = gg.at[k, x, pl.ds(1 - k, 8)]

    @pl.when(off_diag)
    def _():
        rcopy(g_in, own, SEM_T, swap).wait_recv()

    @pl.when(jnp.logical_not(off_diag))
    def _():
        pltpu.make_async_copy(g_in, own, rs.at[SEM_T]).wait()

    landed(gg.at[k, x, 8 * k], SEM_T + 1)
    g_send(1)

    def core_send(i, b):
        push(gg.at[k, b], gg.at[k, b], SEM_C + i, other)

    blocks = (x, mod(x - 1, NX), mod(x + 1, NX), mod(x + 2, NX))
    core_send(0, blocks[0])
    w_recv(1)
    w_send(2)
    x_recv(1)
    x_send(2)
    g_recv(1)
    g_send(2)
    core_send(1, blocks[1])
    core_send(2, blocks[2])
    x_recv(2)
    x_send(3)
    w_recv(2)

    for b in range(NY):
        for i in range(3):
            for j in range(3):
                tap = wg[b, i, j]
                wf[i * 128 + b * 32 : i * 128 + b * 32 + 32, j * 128 : j * 128 + 128] = tap
                wb[j * 128 + b * 32 : j * 128 + b * 32 + 32, i * 128 : i * 128 + 128] = tap

    g_recv(2)
    core_send(3, blocks[3])
    x_recv(3)
    x_send(4)
    for i in range(4):
        landed(gg.at[1 - k, blocks[i]], SEM_C + i)

    col = lax.broadcasted_iota(jnp.int32, (LANES, LANES), 0)

    def shifts(v):
        before = jnp.where(col == 0, 0.0, pltpu.roll(v, 1, 0))
        after = jnp.where(col == LANES - 1, 0.0, pltpu.roll(v, LANES - 1, 0))
        return before.astype(BF16), after.astype(BF16)

    def y_row(q, carry):
        outside = jnp.logical_or(
            jnp.logical_and(q == 0, y == 0), jnp.logical_and(q == 17, y == NY - 1)
        )
        v = gg[lax.div(q, 9), :, lax.rem(q, 9)].reshape(LANES, LANES).astype(F32)
        v = jnp.where(outside, 0.0, v)
        at = pl.multiple_of(q * LANES, LANES)
        dyn[:, pl.ds(at, LANES)] = v.astype(BF16)
        t = v.T
        before, after = shifts(t)
        y3[pl.ds(at, LANES), 0:128] = after
        y3[pl.ds(at, LANES), 128:256] = t.astype(BF16)
        y3[pl.ds(at, LANES), 256:384] = before
        return carry

    lax.fori_loop(0, 18, y_row, 0)

    pdx[0] = jnp.zeros((2, LANES, LANES), F32)

    def dx_pair(t, carry):
        at = pl.multiple_of(t * 2 * LANES, 2 * LANES)
        r = jnp.dot(y3[pl.ds(at, 2 * LANES), :], wb[...], preferred_element_type=F32)
        r0, r1 = r[:LANES], r[LANES:]
        pdx[t, 0] += r0[:, 0:128]
        pdx[t, 1] += r0[:, 128:256] + r1[:, 0:128]
        pdx[t + 1, 0] = r0[:, 256:384] + r1[:, 128:256]
        pdx[t + 1, 1] = r1[:, 256:384]
        return carry

    lax.fori_loop(0, 9, dx_pair, 0)
    dx_send(1)

    x_recv(4)

    def x_row(r, carry):
        v16 = xg[lax.div(r, 2), lax.rem(r, 2)]
        before, after = shifts(v16.astype(F32))
        at = pl.multiple_of(r * LANES, LANES)
        x3[pl.ds(at, LANES), 0:128] = before
        x3[pl.ds(at, LANES), 128:256] = v16
        x3[pl.ds(at, LANES), 256:384] = after
        return carry

    lax.fori_loop(0, 16, x_row, 0)
    dx_advance(1)

    tile = (NX, 2, 16, LANES)
    po[0, :, :, 0] = jnp.zeros(tile, F32)
    po[0, :, :, 1] = jnp.zeros(tile, F32)

    def out_pair(t, carry):
        at = pl.multiple_of(t * 2 * LANES, 2 * LANES)
        r = lax.dot_general(
            wf[...], x3[pl.ds(at, 2 * LANES), :], (((1,), (1,)), ((), ())),
            preferred_element_type=F32,
        )
        r0, r1 = r[:, :LANES], r[:, LANES:]

        def row(q):
            return po.at[lax.div(q, 9), :, :, lax.rem(q, 9)]

        row(2 * t)[...] += r0[256:384].reshape(tile)
        row(2 * t + 1)[...] += (r0[128:256] + r1[256:384]).reshape(tile)
        row(2 * t + 2)[...] = (r0[0:128] + r1[128:256]).reshape(tile)
        row(2 * t + 3)[...] = r1[0:128].reshape(tile)
        return carry

    lax.fori_loop(0, 8, out_pair, 0)
    push(po.at[1 - k], rk, SEM_OC, other)
    dx_advance(2)

    acc[...] = jnp.zeros((384, 384), F32)

    def dw_rows(t, carry):
        at = pl.multiple_of(t * 4 * LANES, 4 * LANES)
        lhs = jnp.concatenate(
            [dyn[:, pl.ds(pl.multiple_of(at + (2 - i) * LANES, LANES), 4 * LANES)] for i in range(3)],
            axis=0,
        )
        acc[...] += jnp.dot(lhs, x3[pl.ds(at, 4 * LANES), :], preferred_element_type=F32)
        return carry

    lax.fori_loop(0, 4, dw_rows, 0)
    for b in range(NY):
        for h in range(2):
            for i in range(3):
                at = i * 128 + b * 32 + h * 16
                pdw[b, h, i] = acc[at : at + 16, :]
    dw_send(1)

    landed(rk, SEM_OC)
    for b in range(NX):
        pk.at[b][...] += rk[b]
    o_send(1)
    dx_advance(3)
    dw_advance(1)
    o_advance(1)

    dw_recv(2)
    for h in range(2):
        for i in range(3):
            total = (pdw[y, h, i] + rdw[0, 1, h, i] + rdw[1, 1, h, i]) * norm
            for j in range(3):
                dw_o[i, j, 16 * h : 16 * h + 16] = total[:, 128 * j : 128 * j + 128]

    o_recv(2)
    mine = po.at[k, x]
    for h in range(2):
        for q in range(9):
            mine[h, q] += ro[0, 1, h, q] + ro[1, 1, h, q]
    push(mine.at[:, 8 * k], rh, SEM_OH, edge)

    dx_recv(4)
    dx_o[...] = (pdx[z + 1] + rdx[0, 3] + rdx[1, 3]).astype(BF16)

    landed(rh, SEM_OH)
    inside = jnp.where(k == 0, y > 0, y < NY - 1)
    for h in range(2):
        mine[h, 1 + 6 * k + (1 - k) * 0] += jnp.where(inside, rh[h], 0.0)
        for q in range(8):
            ob[q, 16 * h : 16 * h + 16] = mine[h, q + 1 - k].astype(BF16)

    @pl.when(off_diag)
    def _():
        rcopy(ob, orx, SEM_OT, swap).start()
        rcopy(ob, orx, SEM_OT, swap).wait_recv()
        out_o[...] = orx[...]
        rcopy(ob, orx, SEM_OT, swap).wait_send()
        rcopy(g_in, main_dst, SEM_T, swap).wait_send()

    @pl.when(jnp.logical_not(off_diag))
    def _():
        out_o[...] = ob[...]

    for copy in sent:
        copy.wait_send()


def body(inputs, weights, cotangent):
    norm = 1.0 / math.sqrt(inputs.shape[0] * cotangent.shape[1] * 8 * inputs.shape[2])
    vmem = pl.BlockSpec(memory_space=pltpu.VMEM)
    out, dx, dw = pl.pallas_call(
        functools.partial(kernel, norm),
        out_shape=(
            jax.ShapeDtypeStruct((8, 32, 128), BF16),
            jax.ShapeDtypeStruct((2, 128, 128), BF16),
            jax.ShapeDtypeStruct((3, 3, 32, 128), F32),
        ),
        in_specs=[vmem] * 3,
        out_specs=[vmem] * 3,
        scratch_shapes=[
            pltpu.VMEM((8, 2, 128, 128), BF16),
            pltpu.VMEM((4, 3, 3, 32, 128), BF16),
            pltpu.VMEM((2, 4, 9, 32, 128), BF16),
            pltpu.VMEM((2048, 384), BF16),
            pltpu.VMEM((2304, 384), BF16),
            pltpu.VMEM((128, 2304), BF16),
            pltpu.VMEM((384, 384), BF16),
            pltpu.VMEM((384, 384), BF16),
            pltpu.VMEM((10, 2, 128, 128), F32),
            pltpu.VMEM((2, 4, 2, 128, 128), F32),
            pltpu.VMEM((384, 384), F32),
            pltpu.VMEM((4, 2, 3, 16, 384), F32),
            pltpu.VMEM((2, 2, 2, 3, 16, 384), F32),
            pltpu.VMEM((2, 4, 2, 9, 16, 128), F32),
            pltpu.VMEM((4, 2, 9, 16, 128), F32),
            pltpu.VMEM((2, 2, 2, 9, 16, 128), F32),
            pltpu.VMEM((2, 16, 128), F32),
            pltpu.VMEM((8, 32, 128), BF16),
            pltpu.VMEM((8, 32, 128), BF16),
            pltpu.SemaphoreType.DMA((N_SEMS,)),
            pltpu.SemaphoreType.DMA((N_SEMS,)),
        ],
        compiler_params=pltpu.CompilerParams(collective_id=0, has_side_effects=True),
        name="conv_layer",
    )(inputs[0], weights, cotangent[0])
    return out[None], dx[None], dw


def solution(mesh):
    return jax.shard_map(
        body,
        mesh=mesh,
        in_specs=(
            P(None, "filt", None, "chan"),
            P(None, None, "filt", "chan"),
            P(None, "chan", "filt", None),
        ),
        out_specs=(
            P(None, "chan", "filt", None),
            P(None, "filt", None, "chan"),
            P(None, None, "filt", "chan"),
        ),
        check_vma=False,
    )
```

time: 369 us -> 62 us (0.17)
  the two profiles are of different devices: /device:TPU:1 before, /device:TPU:5 now
where the time goes in v1:
time: 62 us; the launch traced here: 61.8 us
  Pallas kernels  57.5 us (93%)
  local copies, waits for them, and re-layouts  3.65 us (6%)
  between operations  0.65 us (1%)
    pallas_call x1, Pallas kernels, body(): pl.pallas_call(functools.partial(kernel, norm), out_shape=(jax.ShapeDtype...  57.5 us
    unnamed x5, local copies, waits for them, and re-layouts  3.65 us

profile of v1, /device:TPU:5, one launch (start us, length us, event | category | flops | bytes accessed | tf_op | source)
XLA Modules:
  0.0 61.8 jit_solution(13408946585556167623)
XLA Ops:
  0.6 57.5 %conv_layer.1 = (bf16[8,32,128]{2,1,0:T(8,128)(2,1)}, bf16[2,128,128]{2,1,0:T(8,128)(2,1)}, f32[3,3,32,128]{3,2,1,0:T(8,128)}) custom-call(bf16[2,128,128]{2,1,0:T(8,128)(2,1)} %bitcast.4, bf16[3,3,32,128]{3,2,1,0:T(8,128)(2,1)} %w_in.1, bf16[8,32,128]{2,1,0:T(8,128)(2,1)} %bitcast.5), custom_call_target="tpu_custom_call" | custom-call | tf_op jit(solution)/shard_map/conv_layer/pallas_call | solution.py:375
  58.1 0.0 copy-start
  58.1 1.5 %copy.9 = bf16[1,8,32,128]{3,2,1,0:T(8,128)(2,1)} copy(bf16[1,8,32,128]{3,2,1,0:T(8,128)(2,1)} %bitcast.7) | data formatting | bytes 131072
  59.6 1.5 %copy.10 = bf16[1,2,128,128]{3,2,1,0:T(8,128)(2,1)} copy(bf16[1,2,128,128]{3,2,1,0:T(8,128)(2,1)} %bitcast.6) | data formatting | bytes 131072
  61.1 0.0 copy-done
  61.1 0.7 %copy.11 = f32[3,3,32,128]{3,2,1,0:T(8,128)} copy(f32[3,3,32,128]{3,2,1,0:T(8,128)S(1)} %copy-done) | data formatting | bytes 294912
Async XLA Ops:
  58.1 3.0 %copy-start = (f32[3,3,32,128]{3,2,1,0:T(8,128)S(1)}, f32[3,3,32,128]{3,2,1,0:T(8,128)}, u32[]{:S(2)}) copy-start(f32[3,3,32,128]{3,2,1,0:T(8,128)} %get-tuple-element.14) | copy-start | bytes 442372

commit v2 on v1

v2 whole, which is shorter than its diff:
```python
import functools
import math

import jax
import jax.numpy as jnp
from jax import lax
from jax.experimental import pallas as pl
from jax.experimental.pallas import tpu as pltpu
from jax.sharding import PartitionSpec as P

MESH = pl.DeviceIdType.MESH
BF16 = jnp.bfloat16
F32 = jnp.float32

NX, NY, NZ = 4, 4, 8
LANES = 128

SEM_X = 0
SEM_W = SEM_X + 8
SEM_T = SEM_W + 4
SEM_H = SEM_T + 4
SEM_C = SEM_H + 4
SEM_DX = SEM_C + 4
SEM_DW = SEM_DX + 16
SEM_O = SEM_DW + 8
SEM_OC = SEM_O + 8
SEM_OM = SEM_OC + 1
SEM_OE = SEM_OM + 1
SEM_OH = SEM_OE + 1
N_SEMS = SEM_OH + 1


def kernel(
    norm,
    x_in, w_in, g_in,
    out_o, dx_o, dw_o,
    gin, xg, wg, gg, x3, y3, dyn, wf, wb,
    pdx, rdx, acc, pdw, rdw, po, rk, ro, ob, orx, oe, oh,
    ss, rs, ls,
):
    chan = lax.axis_index("chan")
    filt = lax.axis_index("filt")
    x, k = lax.div(chan, 2), lax.rem(chan, 2)
    y, z = lax.div(filt, NZ), lax.rem(filt, NZ)

    def dev(dx, dk, dy, dz):
        return (dx * 2 + dk, dy * NZ + dz)

    def mod(v, n):
        return lax.rem(v + n, n)

    x_right, x_left = dev(mod(x + 1, NX), k, y, z), dev(mod(x - 1, NX), k, y, z)
    y_right, y_left = dev(x, k, mod(y + 1, NY), z), dev(x, k, mod(y - 1, NY), z)
    z_right, z_left = dev(x, k, y, mod(z + 1, NZ)), dev(x, k, y, mod(z - 1, NZ))
    other = dev(x, 1 - k, y, z)
    swap = dev(y, k, x, z)
    off_diag = x != y
    step = 2 * k - 1
    out_halo_to = dev(mod(y + step, NX), 1 - k, x, z)
    out_halo_from = dev(y, 1 - k, mod(x + step, NY), z)

    loads = [
        pltpu.make_async_copy(g_in, gin, ls.at[0]),
        pltpu.make_async_copy(x_in, xg.at[z], ls.at[1]),
        pltpu.make_async_copy(w_in, wg.at[y], ls.at[2]),
    ]
    for load in loads:
        load.start()

    barrier = pltpu.get_barrier_semaphore()

    def greet(peer):
        pl.semaphore_signal(barrier, inc=1, device_id=peer, device_id_type=MESH)

    for i in range(NY):
        b = mod(y + i, NY)
        greet(dev(mod(y + step, NX), 1 - k, b, z))
        if i:
            greet(dev(y, k, mod(x + i, NY), z))
    for peer in (x_right, x_left, y_right, y_left, z_right, z_left, other, out_halo_from):
        greet(peer)

    @pl.when(off_diag)
    def _():
        greet(swap)

    pdx[...] = jnp.zeros_like(pdx)
    po[...] = jnp.zeros_like(po)
    pl.semaphore_wait(barrier, jnp.where(off_diag, 16, 15))
    for load in loads:
        load.wait()

    sent = []

    def rcopy(src, dst, idx, target):
        return pltpu.make_async_remote_copy(
            src_ref=src, dst_ref=dst, send_sem=ss.at[idx], recv_sem=rs.at[idx],
            device_id=target, device_id_type=MESH,
        )

    def push(src, dst, idx, target):
        copy = rcopy(src, dst, idx, target)
        copy.start()
        sent.append(copy)

    def landed(dst, idx):
        rcopy(dst, dst, idx, other).wait_recv()

    def gather(buf, pos, n, right, left, base, half):
        last = n // 2

        def send(s):
            for d in range(2):
                ref = buf.at[mod(pos - s + 1, n) if d == 0 else mod(pos + s - 1, n)]
                if s == last:
                    ref = half(ref, d)
                push(ref, ref, base + d * last + s - 1, right if d == 0 else left)

        def recv(s):
            for d in range(2):
                ref = buf.at[mod(pos - s, n) if d == 0 else mod(pos + s, n)]
                if s == last:
                    ref = half(ref, d)
                landed(ref, base + d * last + s - 1)

        return send, recv

    def scatter(part, got, pos, n, right, left, base):
        last = n // 2

        def dest(t, d):
            away = last + 1 - t
            return mod(pos + away, n) if d == 0 else mod(pos - away, n)

        def sem(t, d, piece):
            return base + (d * last + t - 1) * 2 + piece

        def send(t, d, piece):
            push(
                part(dest(t, d)).at[piece], got.at[d, t - 1, piece], sem(t, d, piece),
                right if d == 0 else left,
            )

        def start():
            for d in range(2):
                send(1, d, d)

        def start_free():
            for d in range(2):
                send(2, d, 1 - d)

        def advance(t):
            for turn in (1, 0) if t > 1 else (0,):
                for d in range(2):
                    piece = 1 - d if turn else d
                    landed(got.at[d, t - 1, piece], sem(t, d, piece))
                    part(dest(t + 1, d)).at[piece][...] += got[d, t - 1, piece]
                    send(t + 1, d, piece)

        def finish():
            for d in range(2):
                for piece in range(2):
                    landed(got.at[d, last - 1, piece], sem(last, d, piece))

        return start, start_free, advance, finish

    x_send, x_recv = gather(xg, z, NZ, z_right, z_left, SEM_X, lambda ref, d: ref.at[d])
    w_send, w_recv = gather(
        wg, y, NY, y_right, y_left, SEM_W, lambda ref, d: ref.at[:, :, pl.ds(16 * d, 16)]
    )
    dx_start, dx_free, dx_advance, dx_finish = scatter(
        lambda i: pdx.at[i + 1], rdx, z, NZ, z_right, z_left, SEM_DX
    )
    dw_start, dw_free, dw_advance, dw_finish = scatter(
        lambda i: pdw.at[i], rdw, y, NY, y_right, y_left, SEM_DW
    )
    pk = po.at[k]
    o_start, o_free, o_advance, o_finish = scatter(
        lambda i: pk.at[i], ro, x, NX, x_right, x_left, SEM_O
    )

    def main_copy(i):
        target = dev(mod(x + i, NX), k, x, z)
        return pltpu.make_async_remote_copy(
            src_ref=gin, dst_ref=gg.at[k, y, pl.ds(1 - k, 8)],
            send_sem=ss.at[SEM_T + i], recv_sem=rs.at[SEM_T + y],
            device_id=target, device_id_type=MESH,
        )

    def self_copy():
        return pltpu.make_async_copy(gin, gg.at[k, y, pl.ds(1 - k, 8)], ls.at[0])

    for i in (2, 1, 3):
        main_copy(i).start()

    @pl.when(off_diag)
    def _():
        main_copy(0).start()

    @pl.when(jnp.logical_not(off_diag))
    def _():
        self_copy().start()

    x_send(1)
    w_send(1)
    for i in range(NX):
        copy = pltpu.make_async_remote_copy(
            src_ref=gin.at[7 * k], dst_ref=gg.at[1 - k, y, 8 * (1 - k)],
            send_sem=ss.at[SEM_H + i], recv_sem=rs.at[SEM_H + y],
            device_id=dev(mod(x + i, NX), 1 - k, mod(x + step, NY), z), device_id_type=MESH,
        )
        copy.start()
        sent.append(copy)

    w_recv(1)
    w_send(2)
    x_recv(1)
    x_send(2)

    def cot_block(i):
        b = mod(x + i, NY)
        ref = gg.at[k, b, pl.ds(1 - k, 8)]
        if i:
            landed(ref, SEM_T + b)
        else:

            @pl.when(off_diag)
            def _():
                landed(ref, SEM_T + b)

            @pl.when(jnp.logical_not(off_diag))
            def _():
                self_copy().wait()

        landed(gg.at[k, b, 8 * k], SEM_H + b)
        push(gg.at[k, b], gg.at[k, b], SEM_C + i, other)

    for i in (0, 1, 3, 2):
        cot_block(i)
    x_recv(2)
    x_send(3)

    col = lax.broadcasted_iota(jnp.int32, (LANES, LANES), 0)

    def shifts(v):
        before = jnp.where(col == 0, 0.0, pltpu.roll(v, 1, 0))
        after = jnp.where(col == LANES - 1, 0.0, pltpu.roll(v, LANES - 1, 0))
        return before.astype(BF16), after.astype(BF16)

    def y_rows(half):
        def row(ql):
            q = half * 9 + ql
            outside = jnp.logical_or(
                jnp.logical_and(q == 0, y == 0), jnp.logical_and(q == 17, y == NY - 1)
            )
            v = gg[half, :, ql].reshape(LANES, LANES).astype(F32)
            v = jnp.where(outside, 0.0, v)
            at = pl.multiple_of(q * LANES, LANES)
            dyn[:, pl.ds(at, LANES)] = v.astype(BF16)
            t = v.T
            before, after = shifts(t)
            y3[pl.ds(at, LANES), 0:128] = after
            y3[pl.ds(at, LANES), 128:256] = t.astype(BF16)
            y3[pl.ds(at, LANES), 256:384] = before

        def rows(g, carry):
            for u in range(3):
                row(g * 3 + u)
            return carry

        lax.fori_loop(0, 3, rows, 0)

    y_rows(k)
    w_recv(2)
    for b in range(NY):
        for i in range(3):
            for j in range(3):
                tap = wg[b, i, j]
                wf[i * 128 + b * 32 : i * 128 + b * 32 + 32, j * 128 : j * 128 + 128] = tap
                wb[j * 128 + b * 32 : j * 128 + b * 32 + 32, i * 128 : i * 128 + 128] = tap

    for i in (0, 1, 3, 2):
        landed(gg.at[1 - k, mod(x + i, NY)], SEM_C + i)
    y_rows(1 - k)

    far = mod(z + NZ // 2, NZ)

    def dx_pair(i):
        t = mod(far + i, 9)
        at = pl.multiple_of(t * 2 * LANES, 2 * LANES)
        r = jnp.dot(y3[pl.ds(at, 2 * LANES), :], wb[...], preferred_element_type=F32)
        r0, r1 = r[:LANES], r[LANES:]
        pdx[t, 0] += r0[:, 0:128]
        pdx[t, 1] += r0[:, 128:256] + r1[:, 0:128]
        pdx[t + 1, 0] += r0[:, 256:384] + r1[:, 128:256]
        pdx[t + 1, 1] += r1[:, 256:384]

    for i in range(2):
        dx_pair(i)
    dx_start()
    x_recv(3)
    x_send(4)
    for i in range(2, 9):
        dx_pair(i)
    dx_free()

    x_recv(4)

    def x_rows(g, carry):
        for u in range(2):
            v16 = xg[g, u]
            before, after = shifts(v16.astype(F32))
            at = pl.multiple_of((g * 2 + u) * LANES, LANES)
            x3[pl.ds(at, LANES), 0:128] = before
            x3[pl.ds(at, LANES), 128:256] = v16
            x3[pl.ds(at, LANES), 256:384] = after
        return carry

    lax.fori_loop(0, 8, x_rows, 0)

    tile = (NX, 2, 16, LANES)

    def out_pair(i):
        t = (1 - k) * 7 + step * i
        at = pl.multiple_of(t * 2 * LANES, 2 * LANES)
        r = lax.dot_general(
            wf[...], x3[pl.ds(at, 2 * LANES), :], (((1,), (1,)), ((), ())),
            preferred_element_type=F32,
        )
        r0, r1 = r[:, :LANES], r[:, LANES:]

        def row(q):
            return po.at[lax.div(q, 9), :, :, lax.rem(q, 9)]

        row(2 * t)[...] += r0[256:384].reshape(tile)
        row(2 * t + 1)[...] += (r0[128:256] + r1[256:384]).reshape(tile)
        row(2 * t + 2)[...] += (r0[0:128] + r1[128:256]).reshape(tile)
        row(2 * t + 3)[...] += r1[0:128].reshape(tile)

    for i in range(5):
        out_pair(i)
    push(po.at[1 - k], rk, SEM_OC, other)
    dx_advance(1)
    for i in range(5, 8):
        out_pair(i)

    landed(rk, SEM_OC)
    b = mod(x + 2, NX)
    pk.at[b][...] += rk[b]
    o_start()
    for i in (1, 3, 0):
        b = mod(x + i, NX)
        pk.at[b][...] += rk[b]
    o_free()

    def dw_rows(t):
        at = t * 4 * LANES
        lhs = jnp.concatenate(
            [dyn[:, at + (2 - i) * LANES : at + (6 - i) * LANES] for i in range(3)], axis=0
        )
        return jnp.dot(lhs, x3[at : at + 4 * LANES, :], preferred_element_type=F32)

    acc[...] = dw_rows(0)
    acc[...] += dw_rows(1)
    dx_advance(2)
    acc[...] += dw_rows(2)
    acc[...] += dw_rows(3)
    for b in range(NY):
        for h in range(2):
            for i in range(3):
                at = i * 128 + b * 32 + h * 16
                pdw[b, h, i] = acc[at : at + 16, :]
    dw_start()
    dw_free()

    o_advance(1)
    dx_advance(3)
    dw_advance(1)

    o_finish()
    mine = po.at[k, x]
    for h in range(2):
        for q in range(9):
            mine[h, q] += ro[0, 1, h, q] + ro[1, 1, h, q]
    edge = mine.at[:, 7 * k + 1 - k]
    push(mine.at[:, 8 * k], oh, SEM_OH, out_halo_to)
    for h in range(2):
        for q in range(7):
            ob[q, 16 * h : 16 * h + 16] = mine[h, q + 2 * (1 - k)].astype(BF16)

    def out_copies():
        return (rcopy(ob, orx, SEM_OM, swap), rcopy(edge, oe, SEM_OE, swap))

    def out_stays():
        return (
            pltpu.make_async_copy(ob, orx, ls.at[0]), pltpu.make_async_copy(edge, oe, ls.at[1])
        )

    @pl.when(off_diag)
    def _():
        for copy in out_copies():
            copy.start()

    @pl.when(jnp.logical_not(off_diag))
    def _():
        for copy in out_stays():
            copy.start()

    dx_finish()
    dx_o[...] = (pdx[z + 1] + rdx[0, 3] + rdx[1, 3]).astype(BF16)

    dw_finish()
    for h in range(2):
        for i in range(3):
            total = (pdw[y, h, i] + rdw[0, 1, h, i] + rdw[1, 1, h, i]) * norm
            for j in range(3):
                dw_o[i, j, 16 * h : 16 * h + 16] = total[:, 128 * j : 128 * j + 128]

    @pl.when(off_diag)
    def _():
        for copy in out_copies():
            copy.wait()
        main_copy(0).wait_send()

    @pl.when(jnp.logical_not(off_diag))
    def _():
        for copy in out_stays():
            copy.wait()

    landed(oh, SEM_OH)
    inside = jnp.where(k == 0, x > 0, x < NX - 1)
    out_o[pl.ds(1 - k, 7)] = orx[...]
    for h in range(2):
        row = oe[h] + jnp.where(inside, oh[h], 0.0)
        out_o[7 * k, 16 * h : 16 * h + 16] = row.astype(BF16)

    for i in range(1, NX):
        main_copy(i).wait_send()
    for copy in sent:
        copy.wait_send()


def body(inputs, weights, cotangent):
    norm = 1.0 / math.sqrt(inputs.shape[0] * cotangent.shape[1] * 8 * inputs.shape[2])
    vmem = pl.BlockSpec(memory_space=pltpu.VMEM)
    hbm = pl.BlockSpec(memory_space=pl.ANY)
    out, dx, dw = pl.pallas_call(
        functools.partial(kernel, norm),
        out_shape=(
            jax.ShapeDtypeStruct((8, 32, 128), BF16),
            jax.ShapeDtypeStruct((2, 128, 128), BF16),
            jax.ShapeDtypeStruct((3, 3, 32, 128), F32),
        ),
        in_specs=[hbm] * 3,
        out_specs=[vmem] * 3,
        scratch_shapes=[
            pltpu.VMEM((8, 32, 128), BF16),
            pltpu.VMEM((8, 2, 128, 128), BF16),
            pltpu.VMEM((4, 3, 3, 32, 128), BF16),
            pltpu.VMEM((2, 4, 9, 32, 128), BF16),
            pltpu.VMEM((2048, 384), BF16),
            pltpu.VMEM((2304, 384), BF16),
            pltpu.VMEM((128, 2304), BF16),
            pltpu.VMEM((384, 384), BF16),
            pltpu.VMEM((384, 384), BF16),
            pltpu.VMEM((10, 2, 128, 128), F32),
            pltpu.VMEM((2, 4, 2, 128, 128), F32),
            pltpu.VMEM((384, 384), F32),
            pltpu.VMEM((4, 2, 3, 16, 384), F32),
            pltpu.VMEM((2, 2, 2, 3, 16, 384), F32),
            pltpu.VMEM((2, 4, 2, 9, 16, 128), F32),
            pltpu.VMEM((4, 2, 9, 16, 128), F32),
            pltpu.VMEM((2, 2, 2, 9, 16, 128), F32),
            pltpu.VMEM((7, 32, 128), BF16),
            pltpu.VMEM((7, 32, 128), BF16),
            pltpu.VMEM((2, 16, 128), F32),
            pltpu.VMEM((2, 16, 128), F32),
            pltpu.SemaphoreType.DMA((N_SEMS,)),
            pltpu.SemaphoreType.DMA((N_SEMS,)),
            pltpu.SemaphoreType.DMA((3,)),
        ],
        compiler_params=pltpu.CompilerParams(collective_id=0, has_side_effects=True),
        name="conv_layer",
    )(inputs[0], weights, cotangent[0])
    return out[None], dx[None], dw


def solution(mesh):
    return jax.shard_map(
        body,
        mesh=mesh,
        in_specs=(
            P(None, "filt", None, "chan"),
            P(None, None, "filt", "chan"),
            P(None, "chan", "filt", None),
        ),
        out_specs=(
            P(None, "chan", "filt", None),
            P(None, "filt", None, "chan"),
            P(None, None, "filt", "chan"),
        ),
        check_vma=False,
    )
```

time: 62 us -> 49.8 us (0.80)
  the two profiles are of different devices: /device:TPU:5 before, /device:TPU:25 now
where the time goes in v2:
time: 49.8 us; the launch traced here: 49.7 us
  Pallas kernels  45.4 us (91%)
  local copies, waits for them, and re-layouts  3.65 us (7%)
  between operations  0.65 us (1%)
    pallas_call x1, Pallas kernels, body(): pl.pallas_call(functools.partial(kernel, norm), out_shape=(jax.ShapeDtype...  45.4 us
    unnamed x5, local copies, waits for them, and re-layouts  3.65 us

profile of v2, /device:TPU:25, one launch (start us, length us, event | category | flops | bytes accessed | tf_op | source)
XLA Modules:
  0.0 49.7 jit_solution(10112260410225869773)
XLA Ops:
  0.6 45.4 %conv_layer.1 = (bf16[8,32,128]{2,1,0:T(8,128)(2,1)}, bf16[2,128,128]{2,1,0:T(8,128)(2,1)}, f32[3,3,32,128]{3,2,1,0:T(8,128)}) custom-call(bf16[2,128,128]{2,1,0:T(8,128)(2,1)} %bitcast.4, bf16[3,3,32,128]{3,2,1,0:T(8,128)(2,1)} %w_in.1, bf16[8,32,128]{2,1,0:T(8,128)(2,1)} %bitcast.5), custom_call_target="tpu_custom_call" | custom-call | tf_op jit(solution)/shard_map/conv_layer/pallas_call | solution.py:447
  46.0 0.0 copy-start
  46.1 1.5 %copy.9 = bf16[1,8,32,128]{3,2,1,0:T(8,128)(2,1)} copy(bf16[1,8,32,128]{3,2,1,0:T(8,128)(2,1)} %bitcast.7) | data formatting | bytes 131072
  47.6 1.5 %copy.10 = bf16[1,2,128,128]{3,2,1,0:T(8,128)(2,1)} copy(bf16[1,2,128,128]{3,2,1,0:T(8,128)(2,1)} %bitcast.6) | data formatting | bytes 131072
  49.0 0.0 copy-done
  49.0 0.7 %copy.11 = f32[3,3,32,128]{3,2,1,0:T(8,128)} copy(f32[3,3,32,128]{3,2,1,0:T(8,128)S(1)} %copy-done) | data formatting | bytes 294912
Async XLA Ops:
  46.0 3.0 %copy-start = (f32[3,3,32,128]{3,2,1,0:T(8,128)S(1)}, f32[3,3,32,128]{3,2,1,0:T(8,128)}, u32[]{:S(2)}) copy-start(f32[3,3,32,128]{3,2,1,0:T(8,128)} %get-tuple-element.14) | copy-start | bytes 442372

commit v3 on v2

--- a/solution.py
+++ b/solution.py
@@ -16,7 +16,7 @@
 LANES = 128
 
 SEM_X = 0
-SEM_W = SEM_X + 8
+SEM_W = SEM_X + 16
 SEM_T = SEM_W + 4
 SEM_H = SEM_T + 4
 SEM_C = SEM_H + 4
@@ -24,7 +24,7 @@
 SEM_DW = SEM_DX + 16
 SEM_O = SEM_DW + 8
 SEM_OC = SEM_O + 8
-SEM_OM = SEM_OC + 1
+SEM_OM = SEM_OC + 4
 SEM_OE = SEM_OM + 1
 SEM_OH = SEM_OE + 1
 N_SEMS = SEM_OH + 1
@@ -106,24 +106,30 @@
     def landed(dst, idx):
         rcopy(dst, dst, idx, other).wait_recv()
 
-    def gather(buf, pos, n, right, left, base, half):
+    def gather(buf, pos, n, right, left, base, cut, pieces):
         last = n // 2
 
-        def send(s):
-            for d in range(2):
-                ref = buf.at[mod(pos - s + 1, n) if d == 0 else mod(pos + s - 1, n)]
-                if s == last:
-                    ref = half(ref, d)
-                push(ref, ref, base + d * last + s - 1, right if d == 0 else left)
-
-        def recv(s):
-            for d in range(2):
-                ref = buf.at[mod(pos - s, n) if d == 0 else mod(pos + s, n)]
-                if s == last:
-                    ref = half(ref, d)
-                landed(ref, base + d * last + s - 1)
-
-        return send, recv
+        def copy_at(s, d, piece, hops):
+            ref = buf.at[mod(pos - s + hops, n) if d == 0 else mod(pos + s - hops, n)]
+            if pieces == 2 or s == last:
+                ref = cut(ref, piece)
+            return ref, base + ((d * last + s - 1) * pieces + (piece if pieces == 2 else 0))
+
+        def send(s, d, piece):
+            ref, idx = copy_at(s, d, piece, 1)
+            push(ref, ref, idx, right if d == 0 else left)
+
+        def forward(s):
+            for turn in range(pieces if s < last else 1):
+                for d in range(2):
+                    piece = 1 - d if turn else d
+                    if s:
+                        ref, idx = copy_at(s, d, piece, 0)
+                        landed(ref, idx)
+                    if s + 1 < last or s + 1 == last and turn == 0:
+                        send(s + 1, d, piece)
+
+        return forward
 
     def scatter(part, got, pos, n, right, left, base):
         last = n // 2
@@ -149,13 +155,12 @@
             for d in range(2):
                 send(2, d, 1 - d)
 
-        def advance(t):
-            for turn in (1, 0) if t > 1 else (0,):
-                for d in range(2):
-                    piece = 1 - d if turn else d
-                    landed(got.at[d, t - 1, piece], sem(t, d, piece))
-                    part(dest(t + 1, d)).at[piece][...] += got[d, t - 1, piece]
-                    send(t + 1, d, piece)
+        def advance(t, free=False):
+            for d in range(2):
+                piece = 1 - d if free else d
+                landed(got.at[d, t - 1, piece], sem(t, d, piece))
+                part(dest(t + 1, d)).at[piece][...] += got[d, t - 1, piece]
+                send(t + 1, d, piece)
 
         def finish():
             for d in range(2):
@@ -164,9 +169,9 @@
 
         return start, start_free, advance, finish
 
-    x_send, x_recv = gather(xg, z, NZ, z_right, z_left, SEM_X, lambda ref, d: ref.at[d])
-    w_send, w_recv = gather(
-        wg, y, NY, y_right, y_left, SEM_W, lambda ref, d: ref.at[:, :, pl.ds(16 * d, 16)]
+    x_forward = gather(xg, z, NZ, z_right, z_left, SEM_X, lambda ref, d: ref.at[d], 2)
+    w_forward = gather(
+        wg, y, NY, y_right, y_left, SEM_W, lambda ref, d: ref.at[:, :, pl.ds(16 * d, 16)], 1
     )
     dx_start, dx_free, dx_advance, dx_finish = scatter(
         lambda i: pdx.at[i + 1], rdx, z, NZ, z_right, z_left, SEM_DX
@@ -190,6 +195,7 @@
     def self_copy():
         return pltpu.make_async_copy(gin, gg.at[k, y, pl.ds(1 - k, 8)], ls.at[0])
 
+    w_forward(0)
     for i in (2, 1, 3):
         main_copy(i).start()
 
@@ -201,8 +207,6 @@
     def _():
         self_copy().start()
 
-    x_send(1)
-    w_send(1)
     for i in range(NX):
         copy = pltpu.make_async_remote_copy(
             src_ref=gin.at[7 * k], dst_ref=gg.at[1 - k, y, 8 * (1 - k)],
@@ -212,11 +216,6 @@
         copy.start()
         sent.append(copy)
 
-    w_recv(1)
-    w_send(2)
-    x_recv(1)
-    x_send(2)
-
     def cot_block(i):
         b = mod(x + i, NY)
         ref = gg.at[k, b, pl.ds(1 - k, 8)]
@@ -234,11 +233,6 @@
 
         landed(gg.at[k, b, 8 * k], SEM_H + b)
         push(gg.at[k, b], gg.at[k, b], SEM_C + i, other)
-
-    for i in (0, 1, 3, 2):
-        cot_block(i)
-    x_recv(2)
-    x_send(3)
 
     col = lax.broadcasted_iota(jnp.int32, (LANES, LANES), 0)
 
@@ -270,18 +264,15 @@
 
         lax.fori_loop(0, 3, rows, 0)
 
-    y_rows(k)
-    w_recv(2)
-    for b in range(NY):
-        for i in range(3):
-            for j in range(3):
-                tap = wg[b, i, j]
-                wf[i * 128 + b * 32 : i * 128 + b * 32 + 32, j * 128 : j * 128 + 128] = tap
-                wb[j * 128 + b * 32 : j * 128 + b * 32 + 32, i * 128 : i * 128 + 128] = tap
-
-    for i in (0, 1, 3, 2):
-        landed(gg.at[1 - k, mod(x + i, NY)], SEM_C + i)
-    y_rows(1 - k)
+    def x_block(i):
+        block = mod(z + i, NZ)
+        for u in range(2):
+            v16 = xg[block, u]
+            before, after = shifts(v16.astype(F32))
+            at = pl.multiple_of((block * 2 + u) * LANES, LANES)
+            x3[pl.ds(at, LANES), 0:128] = before
+            x3[pl.ds(at, LANES), 128:256] = v16
+            x3[pl.ds(at, LANES), 256:384] = after
 
     far = mod(z + NZ // 2, NZ)
 
@@ -295,33 +286,10 @@
         pdx[t + 1, 0] += r0[:, 256:384] + r1[:, 128:256]
         pdx[t + 1, 1] += r1[:, 256:384]
 
-    for i in range(2):
-        dx_pair(i)
-    dx_start()
-    x_recv(3)
-    x_send(4)
-    for i in range(2, 9):
-        dx_pair(i)
-    dx_free()
-
-    x_recv(4)
-
-    def x_rows(g, carry):
-        for u in range(2):
-            v16 = xg[g, u]
-            before, after = shifts(v16.astype(F32))
-            at = pl.multiple_of((g * 2 + u) * LANES, LANES)
-            x3[pl.ds(at, LANES), 0:128] = before
-            x3[pl.ds(at, LANES), 128:256] = v16
-            x3[pl.ds(at, LANES), 256:384] = after
-        return carry
-
-    lax.fori_loop(0, 8, x_rows, 0)
-
     tile = (NX, 2, 16, LANES)
 
     def out_pair(i):
-        t = (1 - k) * 7 + step * i
+        t = mod(z + i, NZ)
         at = pl.multiple_of(t * 2 * LANES, 2 * LANES)
         r = lax.dot_general(
             wf[...], x3[pl.ds(at, 2 * LANES), :], (((1,), (1,)), ((), ())),
@@ -337,22 +305,6 @@
         row(2 * t + 2)[...] += (r0[0:128] + r1[128:256]).reshape(tile)
         row(2 * t + 3)[...] += r1[0:128].reshape(tile)
 
-    for i in range(5):
-        out_pair(i)
-    push(po.at[1 - k], rk, SEM_OC, other)
-    dx_advance(1)
-    for i in range(5, 8):
-        out_pair(i)
-
-    landed(rk, SEM_OC)
-    b = mod(x + 2, NX)
-    pk.at[b][...] += rk[b]
-    o_start()
-    for i in (1, 3, 0):
-        b = mod(x + i, NX)
-        pk.at[b][...] += rk[b]
-    o_free()
-
     def dw_rows(t):
         at = t * 4 * LANES
         lhs = jnp.concatenate(
@@ -360,9 +312,66 @@
         )
         return jnp.dot(lhs, x3[at : at + 4 * LANES, :], preferred_element_type=F32)
 
+    x_forward(0)
+    x_block(0)
+    x_forward(1)
+    x_block(1)
+    x_block(-1)
+    w_forward(1)
+    x_forward(2)
+    x_block(2)
+    x_block(-2)
+    for i in (0, 1, 3, 2):
+        cot_block(i)
+    y_rows(k)
+    w_forward(2)
+    for b in range(NY):
+        for i in range(3):
+            for j in range(3):
+                tap = wg[b, i, j]
+                wf[i * 128 + b * 32 : i * 128 + b * 32 + 32, j * 128 : j * 128 + 128] = tap
+                wb[j * 128 + b * 32 : j * 128 + b * 32 + 32, i * 128 : i * 128 + 128] = tap
+
+    for i in (0, 1, -1):
+        out_pair(i)
+    for i in (0, 1, 3, 2):
+        landed(gg.at[1 - k, mod(x + i, NY)], SEM_C + i)
+    y_rows(1 - k)
+
+    for i in range(2):
+        dx_pair(i)
+    dx_start()
+    x_forward(3)
+    for i in range(2, 9):
+        dx_pair(i)
+    dx_free()
+    for i in (2, -2):
+        out_pair(i)
+    for i in (3, -3):
+        x_block(i)
+        out_pair(i)
+    x_forward(4)
+    x_block(4)
+    out_pair(4)
+    for i in (2, 1, 3, 0):
+        b = mod(x + i, NX)
+        push(po.at[1 - k, b], rk.at[b], SEM_OC + i, other)
+    dx_advance(1)
     acc[...] = dw_rows(0)
     acc[...] += dw_rows(1)
-    dx_advance(2)
+
+    def core_sum(i):
+        b = mod(x + i, NX)
+        landed(rk.at[b], SEM_OC + i)
+        pk.at[b][...] += rk[b]
+
+    core_sum(2)
+    o_start()
+    for i in (1, 3):
+        core_sum(i)
+    o_free()
+    core_sum(0)
+    dx_advance(2, free=True)
     acc[...] += dw_rows(2)
     acc[...] += dw_rows(3)
     for b in range(NY):
@@ -372,10 +381,11 @@
                 pdw[b, h, i] = acc[at : at + 16, :]
     dw_start()
     dw_free()
-
+    dx_advance(2)
     o_advance(1)
+    dx_advance(3, free=True)
+    dw_advance(1)
     dx_advance(3)
-    dw_advance(1)
 
     o_finish()
     mine = po.at[k, x]
@@ -440,6 +450,15 @@
         copy.wait_send()
 
 
+def place(*refs):
+    sems = refs[6]
+    copies = [pltpu.make_async_copy(refs[i], refs[i + 3], sems.at[i]) for i in range(3)]
+    for copy in copies:
+        copy.start()
+    for copy in copies:
+        copy.wait()
+
+
 def body(inputs, weights, cotangent):
     norm = 1.0 / math.sqrt(inputs.shape[0] * cotangent.shape[1] * 8 * inputs.shape[2])
     vmem = pl.BlockSpec(memory_space=pltpu.VMEM)
@@ -447,9 +466,9 @@
     out, dx, dw = pl.pallas_call(
         functools.partial(kernel, norm),
         out_shape=(
-            jax.ShapeDtypeStruct((8, 32, 128), BF16),
-            jax.ShapeDtypeStruct((2, 128, 128), BF16),
-            jax.ShapeDtypeStruct((3, 3, 32, 128), F32),
+            pltpu.VMEM((8, 32, 128), BF16),
+            pltpu.VMEM((2, 128, 128), BF16),
+            pltpu.VMEM((3, 3, 32, 128), F32),
         ),
         in_specs=[hbm] * 3,
         out_specs=[vmem] * 3,
@@ -482,6 +501,18 @@
         compiler_params=pltpu.CompilerParams(collective_id=0, has_side_effects=True),
         name="conv_layer",
     )(inputs[0], weights, cotangent[0])
+    out, dx, dw = pl.pallas_call(
+        place,
+        out_shape=(
+            jax.ShapeDtypeStruct((8, 32, 128), BF16),
+            jax.ShapeDtypeStruct((2, 128, 128), BF16),
+            jax.ShapeDtypeStruct((3, 3, 32, 128), F32),
+        ),
+        in_specs=[vmem] * 3,
+        out_specs=[hbm] * 3,
+        scratch_shapes=[pltpu.SemaphoreType.DMA((3,))],
+        name="place_results",
+    )(*(pltpu.with_memory_space_constraint(v, pltpu.VMEM) for v in (out, dx, dw)))
     return out[None], dx[None], dw
 
 

time: 49.8 us -> 43.2 us (0.87)
  local copies, waits for them, and re-layouts: 3.65 us -> 0 us
  Pallas kernels: 45.4 us -> 42.5 us
    unnamed x5 -> x0, local copies, waits for them, and re-layouts: 3.65 us -> none
    pallas_call x1 -> x2, Pallas kernels: 45.4 us -> 42.5 us  [the longest x1 41.8 us: body(): pl.pallas_call(functools.partial(kernel, norm), out_shape=(pltpu.VMEM((8,...]
where the time goes in v3:
time: 43.2 us; the launch traced here: 43.1 us
  Pallas kernels  42.5 us (98%)
  between operations  0.64 us (1%)
    pallas_call x1, Pallas kernels, body(): pl.pallas_call(functools.partial(kernel, norm), out_shape=(pltpu.VMEM((8,...  41.8 us

profile of v3, /device:TPU:25, one launch (start us, length us, event | category | flops | bytes accessed | tf_op | source)
XLA Modules:
  0.0 43.1 jit_solution(4219486172406804009)
XLA Ops:
  0.6 41.8 %conv_layer.1 = (bf16[8,32,128]{2,1,0:T(8,128)(2,1)S(1)}, bf16[2,128,128]{2,1,0:T(8,128)(2,1)S(1)}, f32[3,3,32,128]{3,2,1,0:T(8,128)S(1)}) custom-call(bf16[2,128,128]{2,1,0:T(8,128)(2,1)} %bitcast.4, bf16[3,3,32,128]{3,2,1,0:T(8,128)(2,1)} %w_in.1, bf16[8,32,128]{2,1,0:T(8,128)(2,1)} %bitcast.5), custom_call_target="tpu_custom_call" | custom-call | tf_op jit(solution)/shard_map/conv_layer/pallas_call | solution.py:466
  42.4 0.7 %place_results.1 = (bf16[8,32,128]{2,1,0:T(8,128)(2,1)}, bf16[2,128,128]{2,1,0:T(8,128)(2,1)}, f32[3,3,32,128]{3,2,1,0:T(8,128)}) custom-call(bf16[8,32,128]{2,1,0:T(8,128)(2,1)S(1)} %get-tuple-element.9.refs_0_, bf16[2,128,128]{2,1,0:T(8,128)(2,1)S(1)} %get-tuple-element.10.refs_1_, f32[3,3,32,128]{3,2,1,0:T(8,128)S(1)} %get-tuple-element.11.refs_2_), custom_call_target="tpu_custom_call" | custom-call | tf_op jit(solution)/shard_map/place_results/pallas_call | solution.py:504

commit v4 on v3

v4 whole, which is shorter than its diff:
```python
import functools
import math

import jax
import jax.numpy as jnp
from jax import lax
from jax.experimental import pallas as pl
from jax.experimental.pallas import tpu as pltpu
from jax.sharding import PartitionSpec as P

MESH = pl.DeviceIdType.MESH
BF16 = jnp.bfloat16
F32 = jnp.float32

NX, NY, NZ = 4, 4, 8
LANES = 128

PIECES = 4
WAVES = 2


def layout(*sizes):
    return [sum(sizes[:i]) for i in range(len(sizes) + 1)]


Z_RING, X_WAVE, Y_RING = 7 * PIECES, 3 * PIECES // WAVES, 3 * PIECES
R_X, R_W, R_T, R_C, R_DX, R_DW, R_O, R_OC, R_OM, R_OE, R_OH, N_RECV = layout(
    Z_RING, 6, NY, NX, Z_RING, Y_RING, X_WAVE * WAVES, WAVES, WAVES, WAVES, WAVES
)
S_X, S_W, S_T, S_SWAP, S_H, S_C, S_DX, S_DW, S_O, S_OC, S_OM, S_OE, S_OH, N_SEND = layout(*[1] * 13)


def kernel(
    norm,
    x_in, w_in, g_in,
    out_o, dx_o, dw_o,
    out_v, dx_v, dw_v, gin, xg, wg, gg, x3, y3, dyn, wf, wb,
    pdx, rdx, acc, pdw, rdw, po, rk, ro, ob, orx, oe, oh,
    ss, rs, ls, fs,
):
    chan = lax.axis_index("chan")
    filt = lax.axis_index("filt")
    x, k = lax.div(chan, 2), lax.rem(chan, 2)
    y, z = lax.div(filt, NZ), lax.rem(filt, NZ)

    def dev(dx, dk, dy, dz):
        return (dx * 2 + dk, dy * NZ + dz)

    def mod(v, n):
        return lax.rem(v + n, n)

    x_right, x_left = dev(mod(x + 1, NX), k, y, z), dev(mod(x - 1, NX), k, y, z)
    y_right, y_left = dev(x, k, mod(y + 1, NY), z), dev(x, k, mod(y - 1, NY), z)
    z_right, z_left = dev(x, k, y, mod(z + 1, NZ)), dev(x, k, y, mod(z - 1, NZ))
    other = dev(x, 1 - k, y, z)
    swap = dev(y, k, x, z)
    off_diag = x != y
    step = 2 * k - 1
    out_halo_to = dev(mod(y + step, NX), 1 - k, x, z)
    out_halo_from = dev(y, 1 - k, mod(x + step, NY), z)

    loads = [
        pltpu.make_async_copy(g_in, gin, ls.at[0]),
        pltpu.make_async_copy(x_in, xg.at[z], ls.at[1]),
        pltpu.make_async_copy(w_in, wg.at[y], ls.at[2]),
    ]
    for load in loads:
        load.start()

    barrier = pltpu.get_barrier_semaphore()

    def greet(peer):
        pl.semaphore_signal(barrier, inc=1, device_id=peer, device_id_type=MESH)

    for i in range(NY):
        b = mod(y + i, NY)
        greet(dev(mod(y + step, NX), 1 - k, b, z))
        if i:
            greet(dev(y, k, mod(x + i, NY), z))
    for peer in (x_right, x_left, y_right, y_left, z_right, z_left, other, out_halo_from):
        greet(peer)

    @pl.when(off_diag)
    def _():
        greet(swap)

    pdx[...] = jnp.zeros_like(pdx)
    po[...] = jnp.zeros_like(po)
    pl.semaphore_wait(barrier, jnp.where(off_diag, 16, 15))
    for load in loads:
        load.wait()

    def rcopy(src, dst, send, recv, target):
        return pltpu.make_async_remote_copy(
            src_ref=src, dst_ref=dst, send_sem=ss.at[send], recv_sem=rs.at[recv],
            device_id=target, device_id_type=MESH,
        )

    def push(src, dst, send, recv, target):
        rcopy(src, dst, send, recv, target).start()

    def landed(dst, recv):
        rcopy(dst, dst, S_X, recv, other).wait_recv()

    def left_by(size, send):
        rcopy(size, size, send, R_X, other).wait_send()

    def runs(d, pieces, free):
        half = pieces // 2
        first = half if (d == 1) != free else 0
        return range(first, first + half)

    def gather(buf, pos, n, right, left, send_sem, base, cut, pieces):
        last = n // 2

        def piece_at(s, d, piece, hops):
            ref = buf.at[mod(pos - s + hops, n) if d == 0 else mod(pos + s - hops, n)]
            first = runs(d, pieces, False)[0] if s == last else 0
            sem = base + d * (pieces * (last - 1) + pieces // 2) + (s - 1) * pieces + piece - first
            return cut(ref, piece), sem

        def forward(s, free=False):
            for both in zip(runs(0, pieces, free), runs(1, pieces, free)):
                for d in range(2):
                    if s:
                        landed(*piece_at(s, d, both[d], 0))
                    if s + 1 < last or s + 1 == last and not free:
                        ref, recv = piece_at(s + 1, d, both[d], 1)
                        push(ref, ref, send_sem, recv, right if d == 0 else left)

        return forward

    def scatter(part, got, pos, n, right, left, send_sem, base, cut, pieces):
        last = n // 2
        half = pieces // 2

        def dest(t, d):
            away = last + 1 - t
            return mod(pos + away, n) if d == 0 else mod(pos - away, n)

        def sem(t, d, piece):
            first = base + d * (half + pieces * (last - 1))
            if t == 1:
                return first + piece - runs(d, pieces, False)[0]
            return first + half + (t - 2) * pieces + piece

        def each(free):
            for both in zip(runs(0, pieces, free), runs(1, pieces, free)):
                for d in range(2):
                    yield d, both[d]

        def send(t, d, piece):
            push(
                cut(part(dest(t, d)), piece), cut(got.at[d, t - 1], piece), send_sem,
                sem(t, d, piece), right if d == 0 else left,
            )

        def start():
            for d, piece in each(False):
                send(1, d, piece)

        def start_free():
            for d, piece in each(True):
                send(2, d, piece)

        def advance(t, free=False):
            for d, piece in each(free):
                term = cut(got.at[d, t - 1], piece)
                landed(term, sem(t, d, piece))
                cut(part(dest(t + 1, d)), piece)[...] += term[...]
                send(t + 1, d, piece)

        def finish():
            for d in range(2):
                for piece in range(pieces):
                    landed(cut(got.at[d, last - 1], piece), sem(last, d, piece))

        return start, start_free, advance, finish

    def rows_cut(ref, piece):
        return ref.at[piece // 2, pl.ds(64 * (piece % 2), 64)]

    x_forward = gather(xg, z, NZ, z_right, z_left, S_X, R_X, rows_cut, PIECES)
    w_forward = gather(
        wg, y, NY, y_right, y_left, S_W, R_W, lambda ref, i: ref.at[:, :, pl.ds(16 * i, 16)], 2
    )
    dx_start, dx_free, dx_advance, dx_finish = scatter(
        lambda i: pdx.at[i + 1], rdx, z, NZ, z_right, z_left, S_DX, R_DX, rows_cut, PIECES
    )
    dw_start, dw_free, dw_advance, dw_finish = scatter(
        lambda i: pdw.at[i], rdw, y, NY, y_right, y_left, S_DW, R_DW, lambda ref, i: ref.at[i],
        PIECES,
    )
    pk = po.at[k]
    per_wave = PIECES // WAVES
    waves = [
        scatter(
            lambda i: pk.at[i], ro, x, NX, x_right, x_left, S_O, R_O + w * X_WAVE,
            lambda ref, i, first=w * per_wave: ref.at[first + i], per_wave,
        )
        for w in range(WAVES)
    ]

    def main_copy(i):
        return rcopy(
            gin, gg.at[k, y, pl.ds(1 - k, 8)], S_T if i else S_SWAP, R_T + y,
            dev(mod(x + i, NX), k, x, z),
        )

    def self_copy():
        return pltpu.make_async_copy(gin, gg.at[k, y, pl.ds(1 - k, 8)], ls.at[0])

    w_forward(0)
    w_forward(0, free=True)
    for i in (2, 1, 3):
        main_copy(i).start()

    @pl.when(off_diag)
    def _():
        main_copy(0).start()

    @pl.when(jnp.logical_not(off_diag))
    def _():
        self_copy().start()

    for i in range(NX):
        push(
            gin.at[7 * k], gg.at[1 - k, y, 8 * (1 - k)], S_H, R_T + y,
            dev(mod(x + i, NX), 1 - k, mod(x + step, NY), z),
        )

    def cot_block(i):
        b = mod(x + i, NY)
        if i:
            landed(gg.at[k, b], R_T + b)
        else:

            @pl.when(off_diag)
            def _():
                landed(gg.at[k, b], R_T + b)

            @pl.when(jnp.logical_not(off_diag))
            def _():
                landed(gg.at[k, b, 8 * k], R_T + b)
                self_copy().wait()

        push(gg.at[k, b], gg.at[k, b], S_C, R_C + i, other)

    col = lax.broadcasted_iota(jnp.int32, (LANES, LANES), 0)

    def shifts(v):
        before = jnp.where(col == 0, 0.0, pltpu.roll(v, 1, 0))
        after = jnp.where(col == LANES - 1, 0.0, pltpu.roll(v, LANES - 1, 0))
        return before.astype(BF16), after.astype(BF16)

    def y_rows(half):
        def row(ql):
            q = half * 9 + ql
            outside = jnp.logical_or(
                jnp.logical_and(q == 0, y == 0), jnp.logical_and(q == 17, y == NY - 1)
            )
            v = gg[half, :, ql].reshape(LANES, LANES).astype(F32)
            v = jnp.where(outside, 0.0, v)
            at = pl.multiple_of(q * LANES, LANES)
            dyn[:, pl.ds(at, LANES)] = v.astype(BF16)
            t = v.T
            before, after = shifts(t)
            y3[pl.ds(at, LANES), 0:128] = after
            y3[pl.ds(at, LANES), 128:256] = t.astype(BF16)
            y3[pl.ds(at, LANES), 256:384] = before

        def rows(g, carry):
            for u in range(3):
                row(g * 3 + u)
            return carry

        lax.fori_loop(0, 3, rows, 0)

    def x_block(i):
        block = mod(z + i, NZ)
        for u in range(2):
            v16 = xg[block, u]
            before, after = shifts(v16.astype(F32))
            at = pl.multiple_of((block * 2 + u) * LANES, LANES)
            x3[pl.ds(at, LANES), 0:128] = before
            x3[pl.ds(at, LANES), 128:256] = v16
            x3[pl.ds(at, LANES), 256:384] = after

    far = mod(z + NZ // 2, NZ)

    def dx_pair(i):
        t = mod(far + i, 9)
        at = pl.multiple_of(t * 2 * LANES, 2 * LANES)
        r = jnp.dot(y3[pl.ds(at, 2 * LANES), :], wb[...], preferred_element_type=F32)
        r0, r1 = r[:LANES], r[LANES:]
        pdx[t, 0] += r0[:, 0:128]
        pdx[t, 1] += r0[:, 128:256] + r1[:, 0:128]
        pdx[t + 1, 0] += r0[:, 256:384] + r1[:, 128:256]
        pdx[t + 1, 1] += r1[:, 256:384]

    tile = (NX, PIECES, 8, LANES)

    def out_pair(i):
        t = mod(z + i, NZ)
        at = pl.multiple_of(t * 2 * LANES, 2 * LANES)
        r = lax.dot_general(
            wf[...], x3[pl.ds(at, 2 * LANES), :], (((1,), (1,)), ((), ())),
            preferred_element_type=F32,
        )
        r0, r1 = r[:, :LANES], r[:, LANES:]

        def row(q):
            return po.at[lax.div(q, 9), :, :, lax.rem(q, 9)]

        row(2 * t)[...] += r0[256:384].reshape(tile)
        row(2 * t + 1)[...] += (r0[128:256] + r1[256:384]).reshape(tile)
        row(2 * t + 2)[...] += (r0[0:128] + r1[128:256]).reshape(tile)
        row(2 * t + 3)[...] += r1[0:128].reshape(tile)

    def dw_rows(t):
        at = t * 4 * LANES
        lhs = jnp.concatenate(
            [dyn[:, at + (2 - i) * LANES : at + (6 - i) * LANES] for i in range(3)], axis=0
        )
        return jnp.dot(lhs, x3[at : at + 4 * LANES, :], preferred_element_type=F32)

    x_forward(0)
    x_forward(0, free=True)
    x_block(0)
    x_forward(1)
    x_forward(1, free=True)
    x_block(1)
    x_block(-1)
    x_forward(2)
    w_forward(1)
    w_forward(1, free=True)
    x_forward(2, free=True)
    x_block(2)
    x_block(-2)
    for i in (0, 1, 3, 2):
        cot_block(i)
    y_rows(k)
    x_forward(3)
    for i in (0, 1, 3, 2):
        landed(gg.at[1 - k, mod(x + i, NY)], R_C + i)
    y_rows(1 - k)
    w_forward(2)
    for b in range(NY):
        for i in range(3):
            for j in range(3):
                tap = wg[b, i, j]
                wf[i * 128 + b * 32 : i * 128 + b * 32 + 32, j * 128 : j * 128 + 128] = tap
                wb[j * 128 + b * 32 : j * 128 + b * 32 + 32, i * 128 : i * 128 + 128] = tap

    for i in range(2):
        dx_pair(i)
    dx_start()
    for i in (0, 1, -1, 2, -2):
        out_pair(i)
    x_forward(3, free=True)
    for i in (3, -3):
        x_block(i)
        out_pair(i)
    x_forward(4)
    x_block(4)
    out_pair(4)
    for w in range(WAVES):
        mine = pl.ds(w * per_wave, per_wave)
        push(po.at[1 - k, :, mine], rk.at[:, mine], S_OC, R_OC + w, other)
    for i in range(2, 9):
        dx_pair(i)
    dx_free()
    dx_advance(1)

    for w in range(WAVES):
        mine = pl.ds(w * per_wave, per_wave)
        landed(rk.at[:, mine], R_OC + w)
        for i in (2, 1, 3, 0):
            b = mod(x + i, NX)
            pk.at[b, mine][...] += rk[b, w * per_wave : (w + 1) * per_wave]
            if i == 2:
                waves[w][0]()
        waves[w][1]()
    acc[...] = dw_rows(0)
    acc[...] += dw_rows(1)
    acc[...] += dw_rows(2)
    acc[...] += dw_rows(3)
    for b in range(NY):
        for h in range(PIECES):
            for i in range(3):
                at = i * 128 + b * 32 + h * 8
                pdw[b, h, i] = acc[at : at + 8, :]
    dw_start()
    dw_free()
    dx_advance(2, free=True)
    dx_advance(2)
    waves[0][2](1)
    waves[1][2](1)
    dw_advance(1)
    dx_advance(3, free=True)
    dx_advance(3)

    sums = po.at[k, x]

    def out_copies(w):
        edge = sums.at[pl.ds(w * per_wave, per_wave), 7 * k + 1 - k]
        return (ob.at[w], orx.at[w]), (edge, oe.at[w])

    def out_remote(w):
        main, edge = out_copies(w)
        return rcopy(*main, S_OM, R_OM + w, swap), rcopy(*edge, S_OE, R_OE + w, swap)

    def out_local(w):
        main, edge = out_copies(w)
        return (
            pltpu.make_async_copy(*main, ls.at[2 * w]),
            pltpu.make_async_copy(*edge, ls.at[2 * w + 1]),
        )

    def out_wave(w):
        waves[w][3]()
        for h in range(w * per_wave, (w + 1) * per_wave):
            for q in range(9):
                sums[h, q] += ro[0, 1, h, q] + ro[1, 1, h, q]
        push(
            sums.at[pl.ds(w * per_wave, per_wave), 8 * k], oh.at[w], S_OH, R_OH + w, out_halo_to
        )
        for q in range(7):
            pair = sums[w * per_wave : (w + 1) * per_wave, q + 2 * (1 - k)]
            ob[w, q] = pair.reshape(16, LANES).astype(BF16)

        @pl.when(off_diag)
        def _():
            for copy in out_remote(w):
                copy.start()

        @pl.when(jnp.logical_not(off_diag))
        def _():
            for copy in out_local(w):
                copy.start()

    out_wave(0)
    out_wave(1)

    dw_finish()
    for h in range(PIECES):
        for i in range(3):
            total = (pdw[y, h, i] + rdw[0, 1, h, i] + rdw[1, 1, h, i]) * norm
            for j in range(3):
                dw_v[i, j, 8 * h : 8 * h + 8] = total[:, 128 * j : 128 * j + 128]
    stores = [
        pltpu.make_async_copy(dw_v, dw_o, fs.at[0]),
        pltpu.make_async_copy(dx_v, dx_o, fs.at[1]),
        pltpu.make_async_copy(out_v, out_o, fs.at[2]),
    ]
    stores[0].start()

    dx_finish()
    dx_v[...] = (pdx[z + 1] + rdx[0, 3] + rdx[1, 3]).astype(BF16)
    stores[1].start()

    inside = jnp.where(k == 0, x > 0, x < NX - 1)
    for w in range(WAVES):

        @pl.when(off_diag)
        def _():
            for copy in out_remote(w):
                copy.wait_recv()

        @pl.when(jnp.logical_not(off_diag))
        def _():
            for copy in out_local(w):
                copy.wait()

        landed(oh.at[w], R_OH + w)
        out_v[pl.ds(1 - k, 7), 16 * w : 16 * w + 16] = orx[w]
        row = (oe[w] + jnp.where(inside, oh[w], 0.0)).reshape(16, LANES)
        out_v[7 * k, 16 * w : 16 * w + 16] = row.astype(BF16)
    stores[2].start()

    @pl.when(off_diag)
    def _():
        main_copy(0).wait_send()
        left_by(ob, S_OM)
        left_by(oe, S_OE)

    left_by(xg.at[pl.ds(0, 7)], S_X)
    left_by(wg.at[pl.ds(0, 3)], S_W)
    left_by(xg.at[pl.ds(0, 3)], S_T)
    left_by(gin.at[pl.ds(0, 4)], S_H)
    left_by(gg.at[k], S_C)
    left_by(pdx.at[pl.ds(0, 7)], S_DX)
    left_by(pdw.at[pl.ds(0, 3)], S_DW)
    left_by(pk.at[pl.ds(0, 3)], S_O)
    left_by(pk, S_OC)
    left_by(oh, S_OH)
    for store in stores:
        store.wait()


def place(*refs):
    sems = refs[6]
    copies = [pltpu.make_async_copy(refs[i], refs[i + 3], sems.at[i]) for i in range(3)]
    for copy in copies:
        copy.start()
    for copy in copies:
        copy.wait()


def body(inputs, weights, cotangent):
    norm = 1.0 / math.sqrt(inputs.shape[0] * cotangent.shape[1] * 8 * inputs.shape[2])
    vmem = pl.BlockSpec(memory_space=pltpu.VMEM)
    hbm = pl.BlockSpec(memory_space=pl.ANY)
    out, dx, dw = pl.pallas_call(
        functools.partial(kernel, norm),
        out_shape=(
            pltpu.VMEM((8, 32, 128), BF16),
            pltpu.VMEM((2, 128, 128), BF16),
            pltpu.VMEM((3, 3, 32, 128), F32),
        ),
        in_specs=[hbm] * 3,
        out_specs=[hbm] * 3,
        scratch_shapes=[
            pltpu.VMEM((8, 32, 128), BF16),
            pltpu.VMEM((2, 128, 128), BF16),
            pltpu.VMEM((3, 3, 32, 128), F32),
            pltpu.VMEM((8, 32, 128), BF16),
            pltpu.VMEM((8, 2, 128, 128), BF16),
            pltpu.VMEM((4, 3, 3, 32, 128), BF16),
            pltpu.VMEM((2, 4, 9, 32, 128), BF16),
            pltpu.VMEM((2048, 384), BF16),
            pltpu.VMEM((2304, 384), BF16),
            pltpu.VMEM((128, 2304), BF16),
            pltpu.VMEM((384, 384), BF16),
            pltpu.VMEM((384, 384), BF16),
            pltpu.VMEM((10, 2, 128, 128), F32),
            pltpu.VMEM((2, 4, 2, 128, 128), F32),
            pltpu.VMEM((384, 384), F32),
            pltpu.VMEM((4, PIECES, 3, 8, 384), F32),
            pltpu.VMEM((2, 2, PIECES, 3, 8, 384), F32),
            pltpu.VMEM((2, 4, PIECES, 9, 8, 128), F32),
            pltpu.VMEM((4, PIECES, 9, 8, 128), F32),
            pltpu.VMEM((2, 2, PIECES, 9, 8, 128), F32),
            pltpu.VMEM((WAVES, 7, 16, 128), BF16),
            pltpu.VMEM((WAVES, 7, 16, 128), BF16),
            pltpu.VMEM((WAVES, 2, 8, 128), F32),
            pltpu.VMEM((WAVES, 2, 8, 128), F32),
            pltpu.SemaphoreType.DMA((N_SEND,)),
            pltpu.SemaphoreType.DMA((N_RECV,)),
            pltpu.SemaphoreType.DMA((4,)),
            pltpu.SemaphoreType.DMA((3,)),
        ],
        compiler_params=pltpu.CompilerParams(collective_id=0, has_side_effects=True),
        name="conv_layer",
    )(inputs[0], weights, cotangent[0])
    out, dx, dw = pl.pallas_call(
        place,
        out_shape=(
            jax.ShapeDtypeStruct((8, 32, 128), BF16),
            jax.ShapeDtypeStruct((2, 128, 128), BF16),
            jax.ShapeDtypeStruct((3, 3, 32, 128), F32),
        ),
        in_specs=[vmem] * 3,
        out_specs=[hbm] * 3,
        scratch_shapes=[pltpu.SemaphoreType.DMA((3,))],
        name="place_results",
    )(*(pltpu.with_memory_space_constraint(v, pltpu.VMEM) for v in (out, dx, dw)))
    return out[None], dx[None], dw


def solution(mesh):
    return jax.shard_map(
        body,
        mesh=mesh,
        in_specs=(
            P(None, "filt", None, "chan"),
            P(None, None, "filt", "chan"),
            P(None, "chan", "filt", None),
        ),
        out_specs=(
            P(None, "chan", "filt", None),
            P(None, "filt", None, "chan"),
            P(None, None, "filt", "chan"),
        ),
        check_vma=False,
    )
```

time: 43.2 us -> 39.8 us (0.921)
  the two profiles are of different devices: /device:TPU:25 before, /device:TPU:1 now
where the time goes in v4:
time: 39.8 us; the launch traced here: 39.2 us
  Pallas kernels  38.5 us (97%)
  between operations  0.64 us (2%)
    pallas_call x1, Pallas kernels, body(): pl.pallas_call(functools.partial(kernel, norm), out_shape=(pltpu.VMEM((8,...  37.8 us

profile of v4, /device:TPU:1, one launch (start us, length us, event | category | flops | bytes accessed | tf_op | source)
XLA Modules:
  0.0 39.2 jit_solution(3741560819502599333)
XLA Ops:
  0.6 37.8 %conv_layer.1 = (bf16[8,32,128]{2,1,0:T(8,128)(2,1)S(1)}, bf16[2,128,128]{2,1,0:T(8,128)(2,1)S(1)}, f32[3,3,32,128]{3,2,1,0:T(8,128)S(1)}) custom-call(bf16[2,128,128]{2,1,0:T(8,128)(2,1)} %bitcast.4, bf16[3,3,32,128]{3,2,1,0:T(8,128)(2,1)} %w_in.1, bf16[8,32,128]{2,1,0:T(8,128)(2,1)} %bitcast.5), custom_call_target="tpu_custom_call" | custom-call | tf_op jit(solution)/shard_map/conv_layer/pallas_call | solution.py:514
  38.5 0.7 %place_results.1 = (bf16[8,32,128]{2,1,0:T(8,128)(2,1)}, bf16[2,128,128]{2,1,0:T(8,128)(2,1)}, f32[3,3,32,128]{3,2,1,0:T(8,128)}) custom-call(bf16[8,32,128]{2,1,0:T(8,128)(2,1)S(1)} %get-tuple-element.9.refs_0_, bf16[2,128,128]{2,1,0:T(8,128)(2,1)S(1)} %get-tuple-element.10.refs_1_, f32[3,3,32,128]{3,2,1,0:T(8,128)S(1)} %get-tuple-element.11.refs_2_), custom_call_target="tpu_custom_call" | custom-call | tf_op jit(solution)/shard_map/place_results/pallas_call | solution.py:556

commit v5 on v4

--- a/solution.py
+++ b/solution.py
@@ -23,9 +23,9 @@
     return [sum(sizes[:i]) for i in range(len(sizes) + 1)]
 
 
-Z_RING, X_WAVE, Y_RING = 7 * PIECES, 3 * PIECES // WAVES, 3 * PIECES
 R_X, R_W, R_T, R_C, R_DX, R_DW, R_O, R_OC, R_OM, R_OE, R_OH, N_RECV = layout(
-    Z_RING, 6, NY, NX, Z_RING, Y_RING, X_WAVE * WAVES, WAVES, WAVES, WAVES, WAVES
+    12, NY - 1, NY, NX, 2 * (3 * PIECES + PIECES // 2), NY - 1, (NX - 1) * WAVES,
+    WAVES, WAVES, WAVES, WAVES,
 )
 S_X, S_W, S_T, S_SWAP, S_H, S_C, S_DX, S_DW, S_O, S_OC, S_OM, S_OE, S_OH, N_SEND = layout(*[1] * 13)
 
@@ -49,15 +49,28 @@
     def mod(v, n):
         return lax.rem(v + n, n)
 
-    x_right, x_left = dev(mod(x + 1, NX), k, y, z), dev(mod(x - 1, NX), k, y, z)
-    y_right, y_left = dev(x, k, mod(y + 1, NY), z), dev(x, k, mod(y - 1, NY), z)
-    z_right, z_left = dev(x, k, y, mod(z + 1, NZ)), dev(x, k, y, mod(z - 1, NZ))
+    def along_x(i):
+        return dev(mod(x + i, NX), k, y, z)
+
+    def along_y(i):
+        return dev(x, k, mod(y + i, NY), z)
+
+    def along_z(i):
+        return dev(x, k, y, mod(z + i, NZ))
+
     other = dev(x, 1 - k, y, z)
-    swap = dev(y, k, x, z)
     off_diag = x != y
     step = 2 * k - 1
-    out_halo_to = dev(mod(y + step, NX), 1 - k, x, z)
-    out_halo_from = dev(y, 1 - k, mod(x + step, NY), z)
+
+    def owner(i, row):
+        return lax.rem(2 * row + 2 - i + 2 * NX, NX)
+
+    mine = owner(x, y)
+    out_to = dev(y, k, mine, z)
+    out_from = dev(owner(y, x), k, x, z)
+    above, across = mod(y + step, NX), mod(x + step, NY)
+    out_halo_to = dev(above, 1 - k, mine, z)
+    out_halo_from = dev(owner(y, across), 1 - k, across, z)
 
     loads = [
         pltpu.make_async_copy(g_in, gin, ls.at[0]),
@@ -77,16 +90,17 @@
         greet(dev(mod(y + step, NX), 1 - k, b, z))
         if i:
             greet(dev(y, k, mod(x + i, NY), z))
-    for peer in (x_right, x_left, y_right, y_left, z_right, z_left, other, out_halo_from):
+    for peer in (
+        *[along_x(i) for i in (1, 2, 3)], *[along_y(i) for i in (1, 2, 3)],
+        *[along_z(i) for i in (-2, -1, 1, 2)], other, out_from, out_halo_from,
+    ):
         greet(peer)
 
     @pl.when(off_diag)
     def _():
-        greet(swap)
-
-    pdx[...] = jnp.zeros_like(pdx)
-    po[...] = jnp.zeros_like(po)
-    pl.semaphore_wait(barrier, jnp.where(off_diag, 16, 15))
+        greet(dev(y, k, x, z))
+
+    pl.semaphore_wait(barrier, jnp.where(off_diag, 21, 20))
     for load in loads:
         load.wait()
 
@@ -105,101 +119,113 @@
     def left_by(size, send):
         rcopy(size, size, send, R_X, other).wait_send()
 
-    def runs(d, pieces, free):
-        half = pieces // 2
-        first = half if (d == 1) != free else 0
-        return range(first, first + half)
-
-    def gather(buf, pos, n, right, left, send_sem, base, cut, pieces):
-        last = n // 2
-
-        def piece_at(s, d, piece, hops):
-            ref = buf.at[mod(pos - s + hops, n) if d == 0 else mod(pos + s - hops, n)]
-            first = runs(d, pieces, False)[0] if s == last else 0
-            sem = base + d * (pieces * (last - 1) + pieces // 2) + (s - 1) * pieces + piece - first
-            return cut(ref, piece), sem
-
-        def forward(s, free=False):
-            for both in zip(runs(0, pieces, free), runs(1, pieces, free)):
-                for d in range(2):
-                    if s:
-                        landed(*piece_at(s, d, both[d], 0))
-                    if s + 1 < last or s + 1 == last and not free:
-                        ref, recv = piece_at(s + 1, d, both[d], 1)
-                        push(ref, ref, send_sem, recv, right if d == 0 else left)
-
-        return forward
-
-    def scatter(part, got, pos, n, right, left, send_sem, base, cut, pieces):
-        last = n // 2
-        half = pieces // 2
-
-        def dest(t, d):
-            away = last + 1 - t
-            return mod(pos + away, n) if d == 0 else mod(pos - away, n)
-
-        def sem(t, d, piece):
-            first = base + d * (half + pieces * (last - 1))
-            if t == 1:
-                return first + piece - runs(d, pieces, False)[0]
-            return first + half + (t - 2) * pieces + piece
-
-        def each(free):
-            for both in zip(runs(0, pieces, free), runs(1, pieces, free)):
-                for d in range(2):
-                    yield d, both[d]
-
-        def send(t, d, piece):
-            push(
-                cut(part(dest(t, d)), piece), cut(got.at[d, t - 1], piece), send_sem,
-                sem(t, d, piece), right if d == 0 else left,
-            )
-
-        def start():
-            for d, piece in each(False):
-                send(1, d, piece)
-
-        def start_free():
-            for d, piece in each(True):
-                send(2, d, piece)
-
-        def advance(t, free=False):
-            for d, piece in each(free):
-                term = cut(got.at[d, t - 1], piece)
-                landed(term, sem(t, d, piece))
-                cut(part(dest(t + 1, d)), piece)[...] += term[...]
-                send(t + 1, d, piece)
-
-        def finish():
-            for d in range(2):
-                for piece in range(pieces):
-                    landed(cut(got.at[d, last - 1], piece), sem(last, d, piece))
-
-        return start, start_free, advance, finish
-
-    def rows_cut(ref, piece):
+    ways = (1, -1)
+
+    def x_send(d, away, reach, row, slot):
+        ref = xg.at[mod(z - ways[d] * away, NZ), row]
+        push(ref, ref, S_X, R_X + 6 * d + slot, along_z(ways[d] * reach))
+
+    def x_landed(d, away, row, slot):
+        landed(xg.at[mod(z - ways[d] * away, NZ), row], R_X + 6 * d + slot)
+
+    def x_start():
+        for turn in range(2):
+            for d in range(2):
+                x_send(d, 0, 2, d if turn == 0 else 1 - d, turn)
+        for d in range(2):
+            block = xg.at[z]
+            push(block, block, S_X, R_X + 6 * d + 2, along_z(ways[d]))
+
+    def x_relay():
+        for turn in range(2):
+            for d in range(2):
+                row = d if turn == 0 else 1 - d
+                x_landed(d, 2, row, turn)
+                if turn == 0:
+                    x_send(d, 2, 2, row, 3)
+                x_send(d, 2, 1, row, 4 + turn)
+
+    def x_near():
+        for d in range(2):
+            landed(xg.at[mod(z - ways[d], NZ)], R_X + 6 * d + 2)
+
+    def x_third():
+        for turn in range(2):
+            for d in range(2):
+                x_landed(d, 3, d if turn == 0 else 1 - d, 4 + turn)
+
+    def x_fourth():
+        for d in range(2):
+            x_landed(d, 4, d, 3)
+
+    half = PIECES // 2
+    far_pieces = (range(half), range(half, PIECES))
+
+    def dx_cut(ref, piece):
         return ref.at[piece // 2, pl.ds(64 * (piece % 2), 64)]
 
-    x_forward = gather(xg, z, NZ, z_right, z_left, S_X, R_X, rows_cut, PIECES)
-    w_forward = gather(
-        wg, y, NY, y_right, y_left, S_W, R_W, lambda ref, i: ref.at[:, :, pl.ds(16 * i, 16)], 2
-    )
-    dx_start, dx_free, dx_advance, dx_finish = scatter(
-        lambda i: pdx.at[i + 1], rdx, z, NZ, z_right, z_left, S_DX, R_DX, rows_cut, PIECES
-    )
-    dw_start, dw_free, dw_advance, dw_finish = scatter(
-        lambda i: pdw.at[i], rdw, y, NY, y_right, y_left, S_DW, R_DW, lambda ref, i: ref.at[i],
-        PIECES,
-    )
+    def dx_sem(d, stage, piece):
+        return R_DX + d * (3 * PIECES + half) + (piece - d * half if stage == 0 else half + (stage - 1) * PIECES + piece)
+
+    def dx_send(d, away, reach, stage, piece):
+        push(
+            dx_cut(pdx.at[mod(z + ways[d] * away, NZ) + 1], piece),
+            dx_cut(rdx.at[d, stage], piece), S_DX, dx_sem(d, stage, piece),
+            along_z(ways[d] * reach),
+        )
+
+    def dx_order(d):
+        return (*far_pieces[1 - d], *far_pieces[d])
+
+    def dx_fourth():
+        for i in range(half):
+            for d in range(2):
+                dx_send(d, 4, 2, 0, far_pieces[d][i])
+
+    def dx_third():
+        for i in range(PIECES):
+            for d in range(2):
+                dx_send(d, 3, 1, 1, dx_order(d)[i])
+
+    def dx_add(d, away, stage, piece):
+        term = dx_cut(rdx.at[d, stage], piece)
+        landed(term, dx_sem(d, stage, piece))
+        dx_cut(pdx.at[mod(z + ways[d] * away, NZ) + 1], piece)[...] += term[...]
+
+    def dx_second(far):
+        for i in range(half):
+            for d in range(2):
+                piece = far_pieces[d if far else 1 - d][i]
+                dx_add(d, 2, 1, piece)
+                if far:
+                    dx_add(d, 2, 0, piece)
+                dx_send(d, 2, 1, 2, piece)
+
+    def dx_first(far):
+        for i in range(half):
+            for d in range(2):
+                piece = far_pieces[d if far else 1 - d][i]
+                dx_add(d, 1, 2, piece)
+                dx_send(d, 1, 1, 3, piece)
+
+    def dx_finish():
+        for d in range(2):
+            for piece in range(PIECES):
+                landed(dx_cut(rdx.at[d, 3], piece), dx_sem(d, 3, piece))
+
     pk = po.at[k]
     per_wave = PIECES // WAVES
-    waves = [
-        scatter(
-            lambda i: pk.at[i], ro, x, NX, x_right, x_left, S_O, R_O + w * X_WAVE,
-            lambda ref, i, first=w * per_wave: ref.at[first + i], per_wave,
-        )
-        for w in range(WAVES)
-    ]
+    offsets = (2, 1, 3)
+
+    def o_part(w, i):
+        return pk.at[owner(mod(x + i, NX), y), pl.ds(w * per_wave, per_wave)]
+
+    def o_slot(w, i):
+        return ro.at[i - 1, pl.ds(w * per_wave, per_wave)], R_O + w * (NX - 1) + i - 1
+
+    def o_send(w, i):
+        dst, recv = o_slot(w, i)
+        push(o_part(w, i), dst, S_O, recv, along_x(i))
 
     def main_copy(i):
         return rcopy(
@@ -210,8 +236,6 @@
     def self_copy():
         return pltpu.make_async_copy(gin, gg.at[k, y, pl.ds(1 - k, 8)], ls.at[0])
 
-    w_forward(0)
-    w_forward(0, free=True)
     for i in (2, 1, 3):
         main_copy(i).start()
 
@@ -228,6 +252,8 @@
             gin.at[7 * k], gg.at[1 - k, y, 8 * (1 - k)], S_H, R_T + y,
             dev(mod(x + i, NX), 1 - k, mod(x + step, NY), z),
         )
+    for i in offsets:
+        push(wg.at[y], wg.at[y], S_W, R_W + i - 1, along_y(i))
 
     def cot_block(i):
         b = mod(x + i, NY)
@@ -301,7 +327,7 @@
     tile = (NX, PIECES, 8, LANES)
 
     def out_pair(i):
-        t = mod(z + i, NZ)
+        t = (1 - k) * 7 + step * i
         at = pl.multiple_of(t * 2 * LANES, 2 * LANES)
         r = lax.dot_general(
             wf[...], x3[pl.ds(at, 2 * LANES), :], (((1,), (1,)), ((), ())),
@@ -324,27 +350,22 @@
         )
         return jnp.dot(lhs, x3[at : at + 4 * LANES, :], preferred_element_type=F32)
 
-    x_forward(0)
-    x_forward(0, free=True)
+    x_start()
+    pdx[...] = jnp.zeros_like(pdx)
+    po[...] = jnp.zeros_like(po)
     x_block(0)
-    x_forward(1)
-    x_forward(1, free=True)
-    x_block(1)
-    x_block(-1)
-    x_forward(2)
-    w_forward(1)
-    w_forward(1, free=True)
-    x_forward(2, free=True)
-    x_block(2)
-    x_block(-2)
+    x_relay()
     for i in (0, 1, 3, 2):
         cot_block(i)
+    x_near()
+    for i in (1, -1, 2, -2):
+        x_block(i)
     y_rows(k)
-    x_forward(3)
     for i in (0, 1, 3, 2):
         landed(gg.at[1 - k, mod(x + i, NY)], R_C + i)
     y_rows(1 - k)
-    w_forward(2)
+    for i in offsets:
+        landed(wg.at[mod(y - i, NY)], R_W + i - 1)
     for b in range(NY):
         for i in range(3):
             for j in range(3):
@@ -354,33 +375,32 @@
 
     for i in range(2):
         dx_pair(i)
-    dx_start()
-    for i in (0, 1, -1, 2, -2):
-        out_pair(i)
-    x_forward(3, free=True)
+    dx_fourth()
+    x_third()
     for i in (3, -3):
         x_block(i)
+    x_fourth()
+    x_block(4)
+    for i in range(5):
         out_pair(i)
-    x_forward(4)
-    x_block(4)
-    out_pair(4)
     for w in range(WAVES):
-        mine = pl.ds(w * per_wave, per_wave)
-        push(po.at[1 - k, :, mine], rk.at[:, mine], S_OC, R_OC + w, other)
-    for i in range(2, 9):
+        part = pl.ds(w * per_wave, per_wave)
+        push(po.at[1 - k, :, part], rk.at[:, part], S_OC, R_OC + w, other)
+    for i in range(5, 8):
+        out_pair(i)
+    for i in (2, 3, 7, 8):
         dx_pair(i)
-    dx_free()
-    dx_advance(1)
-
+    dx_third()
     for w in range(WAVES):
-        mine = pl.ds(w * per_wave, per_wave)
-        landed(rk.at[:, mine], R_OC + w)
-        for i in (2, 1, 3, 0):
-            b = mod(x + i, NX)
-            pk.at[b, mine][...] += rk[b, w * per_wave : (w + 1) * per_wave]
-            if i == 2:
-                waves[w][0]()
-        waves[w][1]()
+        part = pl.ds(w * per_wave, per_wave)
+        landed(rk.at[:, part], R_OC + w)
+        for i in (*offsets, 0):
+            b = owner(mod(x + i, NX), y)
+            pk.at[b, part][...] += rk[b, w * per_wave : (w + 1) * per_wave]
+            if i:
+                o_send(w, i)
+    for i in (4, 5, 6):
+        dx_pair(i)
     acc[...] = dw_rows(0)
     acc[...] += dw_rows(1)
     acc[...] += dw_rows(2)
@@ -390,62 +410,45 @@
             for i in range(3):
                 at = i * 128 + b * 32 + h * 8
                 pdw[b, h, i] = acc[at : at + 8, :]
-    dw_start()
-    dw_free()
-    dx_advance(2, free=True)
-    dx_advance(2)
-    waves[0][2](1)
-    waves[1][2](1)
-    dw_advance(1)
-    dx_advance(3, free=True)
-    dx_advance(3)
-
-    sums = po.at[k, x]
+    for i in offsets:
+        push(pdw.at[mod(y + i, NY)], rdw.at[i - 1], S_DW, R_DW + i - 1, along_y(i))
+    dx_second(False)
+    dx_second(True)
+    dx_first(False)
+
+    sums = po.at[k, mine]
 
     def out_copies(w):
-        edge = sums.at[pl.ds(w * per_wave, per_wave), 7 * k + 1 - k]
-        return (ob.at[w], orx.at[w]), (edge, oe.at[w])
-
-    def out_remote(w):
-        main, edge = out_copies(w)
-        return rcopy(*main, S_OM, R_OM + w, swap), rcopy(*edge, S_OE, R_OE + w, swap)
-
-    def out_local(w):
-        main, edge = out_copies(w)
+        part = pl.ds(w * per_wave, per_wave)
         return (
-            pltpu.make_async_copy(*main, ls.at[2 * w]),
-            pltpu.make_async_copy(*edge, ls.at[2 * w + 1]),
+            rcopy(ob.at[w], orx.at[w], S_OM, R_OM + w, out_to),
+            rcopy(sums.at[part, 7 * k + 1 - k], oe.at[w], S_OE, R_OE + w, out_to),
+            rcopy(sums.at[part, 8 * k], oh.at[w], S_OH, R_OH + w, out_halo_to),
         )
 
     def out_wave(w):
-        waves[w][3]()
+        for i in offsets:
+            landed(*o_slot(w, i))
         for h in range(w * per_wave, (w + 1) * per_wave):
             for q in range(9):
-                sums[h, q] += ro[0, 1, h, q] + ro[1, 1, h, q]
-        push(
-            sums.at[pl.ds(w * per_wave, per_wave), 8 * k], oh.at[w], S_OH, R_OH + w, out_halo_to
-        )
+                sums[h, q] += ro[0, h, q] + ro[1, h, q] + ro[2, h, q]
+        main, edge, halo = out_copies(w)
+        halo.start()
+        edge.start()
         for q in range(7):
             pair = sums[w * per_wave : (w + 1) * per_wave, q + 2 * (1 - k)]
             ob[w, q] = pair.reshape(16, LANES).astype(BF16)
-
-        @pl.when(off_diag)
-        def _():
-            for copy in out_remote(w):
-                copy.start()
-
-        @pl.when(jnp.logical_not(off_diag))
-        def _():
-            for copy in out_local(w):
-                copy.start()
+        main.start()
 
     out_wave(0)
+    dx_first(True)
     out_wave(1)
 
-    dw_finish()
+    for i in offsets:
+        landed(rdw.at[i - 1], R_DW + i - 1)
     for h in range(PIECES):
         for i in range(3):
-            total = (pdw[y, h, i] + rdw[0, 1, h, i] + rdw[1, 1, h, i]) * norm
+            total = (pdw[y, h, i] + rdw[0, h, i] + rdw[1, h, i] + rdw[2, h, i]) * norm
             for j in range(3):
                 dw_v[i, j, 8 * h : 8 * h + 8] = total[:, 128 * j : 128 * j + 128]
     stores = [
@@ -461,18 +464,8 @@
 
     inside = jnp.where(k == 0, x > 0, x < NX - 1)
     for w in range(WAVES):
-
-        @pl.when(off_diag)
-        def _():
-            for copy in out_remote(w):
-                copy.wait_recv()
-
-        @pl.when(jnp.logical_not(off_diag))
-        def _():
-            for copy in out_local(w):
-                copy.wait()
-
-        landed(oh.at[w], R_OH + w)
+        for copy in out_copies(w):
+            copy.wait_recv()
         out_v[pl.ds(1 - k, 7), 16 * w : 16 * w + 16] = orx[w]
         row = (oe[w] + jnp.where(inside, oh[w], 0.0)).reshape(16, LANES)
         out_v[7 * k, 16 * w : 16 * w + 16] = row.astype(BF16)
@@ -481,9 +474,9 @@
     @pl.when(off_diag)
     def _():
         main_copy(0).wait_send()
-        left_by(ob, S_OM)
-        left_by(oe, S_OE)
-
+
+    left_by(ob, S_OM)
+    left_by(oe, S_OE)
     left_by(xg.at[pl.ds(0, 7)], S_X)
     left_by(wg.at[pl.ds(0, 3)], S_W)
     left_by(xg.at[pl.ds(0, 3)], S_T)
@@ -537,17 +530,17 @@
             pltpu.VMEM((2, 4, 2, 128, 128), F32),
             pltpu.VMEM((384, 384), F32),
             pltpu.VMEM((4, PIECES, 3, 8, 384), F32),
-            pltpu.VMEM((2, 2, PIECES, 3, 8, 384), F32),
+            pltpu.VMEM((3, PIECES, 3, 8, 384), F32),
             pltpu.VMEM((2, 4, PIECES, 9, 8, 128), F32),
             pltpu.VMEM((4, PIECES, 9, 8, 128), F32),
-            pltpu.VMEM((2, 2, PIECES, 9, 8, 128), F32),
+            pltpu.VMEM((3, PIECES, 9, 8, 128), F32),
             pltpu.VMEM((WAVES, 7, 16, 128), BF16),
             pltpu.VMEM((WAVES, 7, 16, 128), BF16),
             pltpu.VMEM((WAVES, 2, 8, 128), F32),
             pltpu.VMEM((WAVES, 2, 8, 128), F32),
             pltpu.SemaphoreType.DMA((N_SEND,)),
             pltpu.SemaphoreType.DMA((N_RECV,)),
-            pltpu.SemaphoreType.DMA((4,)),
+            pltpu.SemaphoreType.DMA((3,)),
             pltpu.SemaphoreType.DMA((3,)),
         ],
         compiler_params=pltpu.CompilerParams(collective_id=0, has_side_effects=True),

time: 39.8 us -> 36.9 us (0.927)
  Pallas kernels: 38.5 us -> 35.8 us
    pallas_call x1, Pallas kernels: 37.8 us -> 35.1 us  [body(): pl.pallas_call(functools.partial(kernel, norm), out_shape=(pltpu.VMEM((8,...]
where the time goes in v5:
time: 36.9 us; the launch traced here: 36.5 us
  Pallas kernels  35.8 us (97%)
  between operations  0.64 us (2%)
    pallas_call x1, Pallas kernels, body(): pl.pallas_call(functools.partial(kernel, norm), out_shape=(pltpu.VMEM((8,...  35.1 us

profile of v5, /device:TPU:1, one launch (start us, length us, event | category | flops | bytes accessed | tf_op | source)
XLA Modules:
  0.0 36.5 jit_solution(8822757887477422136)
XLA Ops:
  0.6 35.1 %conv_layer.1 = (bf16[8,32,128]{2,1,0:T(8,128)(2,1)S(1)}, bf16[2,128,128]{2,1,0:T(8,128)(2,1)S(1)}, f32[3,3,32,128]{3,2,1,0:T(8,128)S(1)}) custom-call(bf16[2,128,128]{2,1,0:T(8,128)(2,1)} %bitcast.4, bf16[3,3,32,128]{3,2,1,0:T(8,128)(2,1)} %w_in.1, bf16[8,32,128]{2,1,0:T(8,128)(2,1)} %bitcast.5), custom_call_target="tpu_custom_call" | custom-call | tf_op jit(solution)/shard_map/conv_layer/pallas_call | solution.py:507
  35.7 0.7 %place_results.1 = (bf16[8,32,128]{2,1,0:T(8,128)(2,1)}, bf16[2,128,128]{2,1,0:T(8,128)(2,1)}, f32[3,3,32,128]{3,2,1,0:T(8,128)}) custom-call(bf16[8,32,128]{2,1,0:T(8,128)(2,1)S(1)} %get-tuple-element.9.refs_0_, bf16[2,128,128]{2,1,0:T(8,128)(2,1)S(1)} %get-tuple-element.10.refs_1_, f32[3,3,32,128]{3,2,1,0:T(8,128)S(1)} %get-tuple-element.11.refs_2_), custom_call_target="tpu_custom_call" | custom-call | tf_op jit(solution)/shard_map/place_results/pallas_call | solution.py:549

commit v6 on v5

--- a/solution.py
+++ b/solution.py
@@ -175,7 +175,7 @@
         )
 
     def dx_order(d):
-        return (*far_pieces[1 - d], *far_pieces[d])
+        return (*far_pieces[d], *far_pieces[1 - d])
 
     def dx_fourth():
         for i in range(half):
@@ -295,12 +295,8 @@
             y3[pl.ds(at, LANES), 128:256] = t.astype(BF16)
             y3[pl.ds(at, LANES), 256:384] = before
 
-        def rows(g, carry):
-            for u in range(3):
-                row(g * 3 + u)
-            return carry
-
-        lax.fori_loop(0, 3, rows, 0)
+        for ql in range(9):
+            row(ql)
 
     def x_block(i):
         block = mod(z + i, NZ)
@@ -324,31 +320,37 @@
         pdx[t + 1, 0] += r0[:, 256:384] + r1[:, 128:256]
         pdx[t + 1, 1] += r1[:, 256:384]
 
-    tile = (NX, PIECES, 8, LANES)
-
-    def out_pair(i):
+    tile = (NX, PIECES // WAVES, 8, LANES)
+
+    def out_pair(i, w):
         t = (1 - k) * 7 + step * i
         at = pl.multiple_of(t * 2 * LANES, 2 * LANES)
         r = lax.dot_general(
-            wf[...], x3[pl.ds(at, 2 * LANES), :], (((1,), (1,)), ((), ())),
+            wf[192 * w : 192 * w + 192], x3[pl.ds(at, 2 * LANES), :], (((1,), (1,)), ((), ())),
             preferred_element_type=F32,
         )
         r0, r1 = r[:, :LANES], r[:, LANES:]
 
         def row(q):
-            return po.at[lax.div(q, 9), :, :, lax.rem(q, 9)]
-
-        row(2 * t)[...] += r0[256:384].reshape(tile)
-        row(2 * t + 1)[...] += (r0[128:256] + r1[256:384]).reshape(tile)
-        row(2 * t + 2)[...] += (r0[0:128] + r1[128:256]).reshape(tile)
-        row(2 * t + 3)[...] += r1[0:128].reshape(tile)
-
-    def dw_rows(t):
-        at = t * 4 * LANES
+            return po.at[lax.div(q, 9), :, pl.ds(w * per_wave, per_wave), lax.rem(q, 9)]
+
+        row(2 * t)[...] += r0[128:192].reshape(tile)
+        row(2 * t + 1)[...] += (r0[64:128] + r1[128:192]).reshape(tile)
+        row(2 * t + 2)[...] += (r0[0:64] + r1[64:128]).reshape(tile)
+        row(2 * t + 3)[...] += r1[0:64].reshape(tile)
+
+    def dw_all():
         lhs = jnp.concatenate(
-            [dyn[:, at + (2 - i) * LANES : at + (6 - i) * LANES] for i in range(3)], axis=0
-        )
-        return jnp.dot(lhs, x3[at : at + 4 * LANES, :], preferred_element_type=F32)
+            [dyn[:, (2 - i) * LANES : (18 - i) * LANES] for i in range(3)], axis=0
+        )
+        acc[...] = jnp.dot(lhs, x3[...], preferred_element_type=F32)
+        for b in range(NY):
+            for i in range(3):
+                pdw[b, i] = acc[128 * i + 32 * b : 128 * i + 32 * b + 32, :]
+        for away in offsets:
+            push(
+                pdw.at[mod(y + away, NY)], rdw.at[away - 1], S_DW, R_DW + away - 1, along_y(away)
+            )
 
     x_start()
     pdx[...] = jnp.zeros_like(pdx)
@@ -370,28 +372,31 @@
         for i in range(3):
             for j in range(3):
                 tap = wg[b, i, j]
-                wf[i * 128 + b * 32 : i * 128 + b * 32 + 32, j * 128 : j * 128 + 128] = tap
+                for w in range(WAVES):
+                    at = w * 192 + i * 64 + b * 16
+                    wf[at : at + 16, j * 128 : j * 128 + 128] = tap[16 * w : 16 * w + 16]
                 wb[j * 128 + b * 32 : j * 128 + b * 32 + 32, i * 128 : i * 128 + 128] = tap
 
-    for i in range(2):
+    for i in (0, 1):
         dx_pair(i)
     dx_fourth()
+    for i in (2, 3, 7, 8):
+        dx_pair(i)
+    dx_third()
     x_third()
     for i in (3, -3):
         x_block(i)
     x_fourth()
     x_block(4)
-    for i in range(5):
-        out_pair(i)
     for w in range(WAVES):
+        for i in range(5):
+            out_pair(i, w)
         part = pl.ds(w * per_wave, per_wave)
         push(po.at[1 - k, :, part], rk.at[:, part], S_OC, R_OC + w, other)
-    for i in range(5, 8):
-        out_pair(i)
-    for i in (2, 3, 7, 8):
-        dx_pair(i)
-    dx_third()
     for w in range(WAVES):
+        for i in range(5, 8):
+            out_pair(i, w)
+    def core_sum(w):
         part = pl.ds(w * per_wave, per_wave)
         landed(rk.at[:, part], R_OC + w)
         for i in (*offsets, 0):
@@ -399,22 +404,14 @@
             pk.at[b, part][...] += rk[b, w * per_wave : (w + 1) * per_wave]
             if i:
                 o_send(w, i)
+
+    core_sum(0)
     for i in (4, 5, 6):
         dx_pair(i)
-    acc[...] = dw_rows(0)
-    acc[...] += dw_rows(1)
-    acc[...] += dw_rows(2)
-    acc[...] += dw_rows(3)
-    for b in range(NY):
-        for h in range(PIECES):
-            for i in range(3):
-                at = i * 128 + b * 32 + h * 8
-                pdw[b, h, i] = acc[at : at + 8, :]
-    for i in offsets:
-        push(pdw.at[mod(y + i, NY)], rdw.at[i - 1], S_DW, R_DW + i - 1, along_y(i))
+    core_sum(1)
+    dw_all()
+    dx_second(True)
     dx_second(False)
-    dx_second(True)
-    dx_first(False)
 
     sums = po.at[k, mine]
 
@@ -442,15 +439,14 @@
 
     out_wave(0)
     dx_first(True)
+    dx_first(False)
     out_wave(1)
-
-    for i in offsets:
-        landed(rdw.at[i - 1], R_DW + i - 1)
-    for h in range(PIECES):
-        for i in range(3):
-            total = (pdw[y, h, i] + rdw[0, h, i] + rdw[1, h, i] + rdw[2, h, i]) * norm
-            for j in range(3):
-                dw_v[i, j, 8 * h : 8 * h + 8] = total[:, 128 * j : 128 * j + 128]
+    for away in offsets:
+        landed(rdw.at[away - 1], R_DW + away - 1)
+    for i in range(3):
+        total = (pdw[y, i] + rdw[0, i] + rdw[1, i] + rdw[2, i]) * norm
+        for j in range(3):
+            dw_v[i, j] = total[:, 128 * j : 128 * j + 128]
     stores = [
         pltpu.make_async_copy(dw_v, dw_o, fs.at[0]),
         pltpu.make_async_copy(dx_v, dx_o, fs.at[1]),
@@ -529,8 +525,8 @@
             pltpu.VMEM((10, 2, 128, 128), F32),
             pltpu.VMEM((2, 4, 2, 128, 128), F32),
             pltpu.VMEM((384, 384), F32),
-            pltpu.VMEM((4, PIECES, 3, 8, 384), F32),
-            pltpu.VMEM((3, PIECES, 3, 8, 384), F32),
+            pltpu.VMEM((4, 3, 32, 384), F32),
+            pltpu.VMEM((3, 3, 32, 384), F32),
             pltpu.VMEM((2, 4, PIECES, 9, 8, 128), F32),
             pltpu.VMEM((4, PIECES, 9, 8, 128), F32),
             pltpu.VMEM((3, PIECES, 9, 8, 128), F32),

time: 36.9 us -> 36.3 us (0.984)
  Pallas kernels: 35.8 us -> 35.4 us
    pallas_call x1, Pallas kernels: 35.1 us -> 34.6 us  [body(): pl.pallas_call(functools.partial(kernel, norm), out_shape=(pltpu.VMEM((8,...]
where the time goes in v6:
time: 36.3 us; the launch traced here: 36 us
  Pallas kernels  35.4 us (98%)
  between operations  0.64 us (2%)
    pallas_call x1, Pallas kernels, body(): pl.pallas_call(functools.partial(kernel, norm), out_shape=(pltpu.VMEM((8,...  34.6 us
    pallas_call x1, Pallas kernels, body(): pl.pallas_call(place, out_shape=(jax.ShapeDtypeStruct((8, 32, 128), BF16)...  0.73 us

profile of v6, /device:TPU:1, one launch (start us, length us, event | category | flops | bytes accessed | tf_op | source)
XLA Modules:
  0.0 36.0 jit_solution(6138933000621084658)
XLA Ops:
  0.6 34.6 %conv_layer.1 = (bf16[8,32,128]{2,1,0:T(8,128)(2,1)S(1)}, bf16[2,128,128]{2,1,0:T(8,128)(2,1)S(1)}, f32[3,3,32,128]{3,2,1,0:T(8,128)S(1)}) custom-call(bf16[2,128,128]{2,1,0:T(8,128)(2,1)} %bitcast.4, bf16[3,3,32,128]{3,2,1,0:T(8,128)(2,1)} %w_in.1, bf16[8,32,128]{2,1,0:T(8,128)(2,1)} %bitcast.5), custom_call_target="tpu_custom_call" | custom-call | tf_op jit(solution)/shard_map/conv_layer/pallas_call | solution.py:503
  35.3 0.7 %place_results.1 = (bf16[8,32,128]{2,1,0:T(8,128)(2,1)}, bf16[2,128,128]{2,1,0:T(8,128)(2,1)}, f32[3,3,32,128]{3,2,1,0:T(8,128)}) custom-call(bf16[8,32,128]{2,1,0:T(8,128)(2,1)S(1)} %get-tuple-element.9.refs_0_, bf16[2,128,128]{2,1,0:T(8,128)(2,1)S(1)} %get-tuple-element.10.refs_1_, f32[3,3,32,128]{3,2,1,0:T(8,128)S(1)} %get-tuple-element.11.refs_2_), custom_call_target="tpu_custom_call" | custom-call | tf_op jit(solution)/shard_map/place_results/pallas_call | solution.py:545

commit v7 on v6

--- a/solution.py
+++ b/solution.py
@@ -63,7 +63,8 @@
     step = 2 * k - 1
 
     def owner(i, row):
-        return lax.rem(2 * row + 2 - i + 2 * NX, NX)
+        inner = lax.div(row * (NY - 1 - row), 2)
+        return lax.rem(inner * (2 * row + 2 - i) + (1 - inner) * (i + 2) + 2 * NX, NX)
 
     mine = owner(x, y)
     out_to = dev(y, k, mine, z)
@@ -85,7 +86,7 @@
     def greet(peer):
         pl.semaphore_signal(barrier, inc=1, device_id=peer, device_id_type=MESH)
 
-    for i in range(NY):
+    for i in (2, 1, 3, 0):
         b = mod(y + i, NY)
         greet(dev(mod(y + step, NX), 1 - k, b, z))
         if i:

time: 36.3 us -> 36 us (level)
  no operation moved by 1% of the time
where the time goes in v7:
time: 36 us; the launch traced here: 35.9 us
  Pallas kernels  35.2 us (98%)
  between operations  0.64 us (2%)
    pallas_call x1, Pallas kernels, body(): pl.pallas_call(functools.partial(kernel, norm), out_shape=(pltpu.VMEM((8,...  34.5 us
    pallas_call x1, Pallas kernels, body(): pl.pallas_call(place, out_shape=(jax.ShapeDtypeStruct((8, 32, 128), BF16)...  0.73 us

profile of v7, /device:TPU:1, one launch (start us, length us, event | category | flops | bytes accessed | tf_op | source)
XLA Modules:
  0.0 35.9 jit_solution(11098985932028103745)
XLA Ops:
  0.6 34.5 %conv_layer.1 = (bf16[8,32,128]{2,1,0:T(8,128)(2,1)S(1)}, bf16[2,128,128]{2,1,0:T(8,128)(2,1)S(1)}, f32[3,3,32,128]{3,2,1,0:T(8,128)S(1)}) custom-call(bf16[2,128,128]{2,1,0:T(8,128)(2,1)} %bitcast.4, bf16[3,3,32,128]{3,2,1,0:T(8,128)(2,1)} %w_in.1, bf16[8,32,128]{2,1,0:T(8,128)(2,1)} %bitcast.5), custom_call_target="tpu_custom_call" | custom-call | tf_op jit(solution)/shard_map/conv_layer/pallas_call | solution.py:504
  35.1 0.7 %place_results.1 = (bf16[8,32,128]{2,1,0:T(8,128)(2,1)}, bf16[2,128,128]{2,1,0:T(8,128)(2,1)}, f32[3,3,32,128]{3,2,1,0:T(8,128)}) custom-call(bf16[8,32,128]{2,1,0:T(8,128)(2,1)S(1)} %get-tuple-element.9.refs_0_, bf16[2,128,128]{2,1,0:T(8,128)(2,1)S(1)} %get-tuple-element.10.refs_1_, f32[3,3,32,128]{3,2,1,0:T(8,128)S(1)} %get-tuple-element.11.refs_2_), custom_call_target="tpu_custom_call" | custom-call | tf_op jit(solution)/shard_map/place_results/pallas_call | solution.py:546

commit v8 on v7

--- a/solution.py
+++ b/solution.py
@@ -27,7 +27,10 @@
     12, NY - 1, NY, NX, 2 * (3 * PIECES + PIECES // 2), NY - 1, (NX - 1) * WAVES,
     WAVES, WAVES, WAVES, WAVES,
 )
-S_X, S_W, S_T, S_SWAP, S_H, S_C, S_DX, S_DW, S_O, S_OC, S_OM, S_OE, S_OH, N_SEND = layout(*[1] * 13)
+S_SWAP, S_X, S_C, S_DX, N_SEND = range(5)
+S_W = S_OM = S_X
+S_DW = S_O = S_OC = S_C
+S_T = S_H = S_OE = S_OH = S_DX
 
 
 def kernel(
@@ -176,7 +179,7 @@
         )
 
     def dx_order(d):
-        return (*far_pieces[d], *far_pieces[1 - d])
+        return (*far_pieces[1 - d], *far_pieces[d])
 
     def dx_fourth():
         for i in range(half):
@@ -411,8 +414,8 @@
         dx_pair(i)
     core_sum(1)
     dw_all()
+    dx_second(False)
     dx_second(True)
-    dx_second(False)
 
     sums = po.at[k, mine]
 
@@ -439,8 +442,8 @@
         main.start()
 
     out_wave(0)
+    dx_first(False)
     dx_first(True)
-    dx_first(False)
     out_wave(1)
     for away in offsets:
         landed(rdw.at[away - 1], R_DW + away - 1)
@@ -472,18 +475,9 @@
     def _():
         main_copy(0).wait_send()
 
-    left_by(ob, S_OM)
-    left_by(oe, S_OE)
-    left_by(xg.at[pl.ds(0, 7)], S_X)
-    left_by(wg.at[pl.ds(0, 3)], S_W)
-    left_by(xg.at[pl.ds(0, 3)], S_T)
-    left_by(gin.at[pl.ds(0, 4)], S_H)
-    left_by(gg.at[k], S_C)
-    left_by(pdx.at[pl.ds(0, 7)], S_DX)
-    left_by(pdw.at[pl.ds(0, 3)], S_DW)
-    left_by(pk.at[pl.ds(0, 3)], S_O)
-    left_by(pk, S_OC)
-    left_by(oh, S_OH)
+    left_by(y3.at[pl.ds(0, 960)], S_X)
+    left_by(y3, S_C)
+    left_by(pdx.at[pl.ds(0, 9)], S_DX)
     for store in stores:
         store.wait()
 

time: 36 us -> 35.9 us (level)
  no operation moved by 1% of the time
where the time goes in v8:
time: 35.9 us; the launch traced here: 35.8 us
  Pallas kernels  35.1 us (98%)
  between operations  0.64 us (2%)
    pallas_call x1, Pallas kernels, body(): pl.pallas_call(functools.partial(kernel, norm), out_shape=(pltpu.VMEM((8,...  34.4 us
    pallas_call x1, Pallas kernels, body(): pl.pallas_call(place, out_shape=(jax.ShapeDtypeStruct((8, 32, 128), BF16)...  0.73 us

profile of v8, /device:TPU:1, one launch (start us, length us, event | category | flops | bytes accessed | tf_op | source)
XLA Modules:
  0.0 35.8 jit_solution(15153175801305967246)
XLA Ops:
  0.6 34.4 %conv_layer.1 = (bf16[8,32,128]{2,1,0:T(8,128)(2,1)S(1)}, bf16[2,128,128]{2,1,0:T(8,128)(2,1)S(1)}, f32[3,3,32,128]{3,2,1,0:T(8,128)S(1)}) custom-call(bf16[2,128,128]{2,1,0:T(8,128)(2,1)} %bitcast.4, bf16[3,3,32,128]{3,2,1,0:T(8,128)(2,1)} %w_in.1, bf16[8,32,128]{2,1,0:T(8,128)(2,1)} %bitcast.5), custom_call_target="tpu_custom_call" | custom-call | tf_op jit(solution)/shard_map/conv_layer/pallas_call | solution.py:498
  35.1 0.7 %place_results.1 = (bf16[8,32,128]{2,1,0:T(8,128)(2,1)}, bf16[2,128,128]{2,1,0:T(8,128)(2,1)}, f32[3,3,32,128]{3,2,1,0:T(8,128)}) custom-call(bf16[8,32,128]{2,1,0:T(8,128)(2,1)S(1)} %get-tuple-element.9.refs_0_, bf16[2,128,128]{2,1,0:T(8,128)(2,1)S(1)} %get-tuple-element.10.refs_1_, f32[3,3,32,128]{3,2,1,0:T(8,128)S(1)} %get-tuple-element.11.refs_2_), custom_call_target="tpu_custom_call" | custom-call | tf_op jit(solution)/shard_map/place_results/pallas_call | solution.py:540
